TPU v7x, 32 devices: a whole 2x2x4 slice. The times are simulated.
32 devices in a mesh: section: 2 (over x), dp: 16 (over z, y, core).
Axes of the slice: x: 2, y: 2, z: 4, core: 2. Of those that a mesh axis runs over, the one named last changes fastest.
Arguments:
- inputs: bfloat16 [2, 16, 256, 768], P(None, 'dp'), may hold values from -6 to 6
- clip_lengths: int32 [2, 16, 4], P(None, 'dp'), may hold values from 1 to 128, 256 in all within a row
- anchor_offsets: int32 [2, 16, 4], P(None, 'dp'), may hold values from 0 to 63
- cotangent: bfloat16 [2, 16, 256, 768], P(None, 'dp'), may hold values from -6 to 6
- inward_weight: bfloat16 [2, 768, 2304], P('section'), may hold values from -0.3125 to 0.3125
- outward_weight: bfloat16 [2, 768, 768], P('section'), may hold values from -0.625 to 0.625
- up_weight: bfloat16 [2, 768, 3072], P('section'), may hold values from -0.21875 to 0.21875
- down_weight: bfloat16 [2, 3072, 768], P('section'), may hold values from -0.15625 to 0.15625
- norm_gain: float32 [2, 2, 768], P('section'), may hold values from 0.1 to 1.9
- norm_bias: float32 [2, 2, 768], P('section'), may hold values from -3 to 3
Outputs:
- layer_outputs: bfloat16 [2, 2, 16, 256, 768], P('section', None, 'dp')
- input_grads: float32 [2, 2, 16, 256, 768], P('section', None, 'dp')
- inward_grad: float32 [2, 768, 2304], P('section', 'dp')
- outward_grad: float32 [2, 768, 768], P('section', 'dp')
- up_grad: float32 [2, 768, 3072], P('section', 'dp')
- down_grad: float32 [2, 3072, 768], P('section', 'dp')
- gain_grad: float32 [2, 2, 768], P('section', None, 'dp')
- bias_grad: float32 [2, 2, 768], P('section', None, 'dp')
Inputs may be any that keep to these rules, and one draw needn't show every extreme that they name: `clip_lengths`: in each sequence the 4 clip lengths sum to 256, and the longest is half of 256.
All inputs are finite; a program needn't handle non-finite values.
Results may differ from a plain program's by a relative error of at most 0.025.
Values may be sent and summed in bfloat16 or wider, within the bound.
A program may use at most 320 MiB of HBM per device.

v0:
```python
import jax
import jax.numpy as jnp
from jax import lax
from jax.sharding import PartitionSpec as P

HEAD = 64


EPSILON = 1e-06


def shifted(x, axis, by):
    size = lax.axis_size(axis)
    pairs = [(i, i + by) for i in range(size) if 0 <= i + by < size]
    return lax.ppermute(x, axis, pairs)


def norm_rows(values, norm_gain, norm_bias):
    average = jnp.mean(values, -1, keepdims=True)
    centred = values - average
    inverse = lax.rsqrt(jnp.mean(centred * centred, -1, keepdims=True) + EPSILON)
    normed = centred * inverse
    return (normed * norm_gain + norm_bias, normed, inverse)


def norm_back(norm_grad, normed, inverse, norm_gain):
    inner = norm_grad * norm_gain
    through = inverse * (
        inner
        - jnp.mean(inner, -1, keepdims=True)
        - normed * jnp.mean(inner * normed, -1, keepdims=True)
    )
    return (through, jnp.sum(norm_grad * normed, 0), jnp.sum(norm_grad, 0))


def gelu_slope(lifted):
    cumulative = 0.5 * (1.0 + lax.erf(lifted * 0.7071067811865476))
    density = jnp.exp(-0.5 * lifted * lifted) * 0.3989422804014327
    return cumulative + lifted * density


def clip_marks(lengths, offsets, length):
    positions = jnp.arange(length, dtype=jnp.int32)
    clip_ends = jnp.cumsum(lengths)
    clip_starts = clip_ends - lengths
    anchor_at = clip_starts + offsets % lengths
    clip_ids = jnp.sum((positions[:, None] >= clip_ends[None, :]).astype(jnp.int32), 1)
    anchors = jnp.any(positions[:, None] == anchor_at[None, :], 1)
    return (clip_ids, anchors)


def masked_scores(query_block, key_rows, id_block, clip_ids, anchors, scaling):
    scores = (
        jnp.einsum("qhd,khd->hqk", query_block, key_rows, preferred_element_type=jnp.float32)
        * scaling
    )
    seen = (id_block[:, None] == clip_ids[None, :]) | anchors[None, :]
    return jnp.where(seen[None], scores, -1000000000.0)


def forward_layer(source, clip_ids, anchors, params):
    inward, outward, upward, downward, norm_gain, norm_bias = params
    length, model_width = source.shape
    head_count = model_width // HEAD
    scaling = HEAD ** (-0.5)
    residual = source.astype(jnp.float32)
    first_norm, unit_one, scale_one = norm_rows(residual, norm_gain[0], norm_bias[0])
    joined = jnp.dot(
        first_norm.astype(jnp.bfloat16), inward, preferred_element_type=jnp.float32
    ).astype(jnp.bfloat16)
    heads_view = joined.reshape(length, 3, head_count, HEAD)
    queries = heads_view[:, 0]
    key_rows = heads_view[:, 1]
    values = heads_view[:, 2]
    scores = masked_scores(queries, key_rows, clip_ids, clip_ids, anchors, scaling)
    row_max = jnp.max(scores, -1, keepdims=True)
    raised = jnp.exp(scores - row_max)
    row_sum = jnp.sum(raised, -1, keepdims=True)
    weights = (raised / row_sum).astype(jnp.bfloat16)
    pieces = [jnp.einsum("hqk,khd->qhd", weights, values, preferred_element_type=jnp.float32)]
    log_sums = [(row_max + jnp.log(row_sum))[..., 0]]
    attended = jnp.concatenate(pieces, 0).reshape(length, model_width).astype(jnp.bfloat16)
    logsum = jnp.concatenate(log_sums, 1)
    middle = residual + jnp.dot(attended, outward, preferred_element_type=jnp.float32)
    second_norm, unit_two, scale_two = norm_rows(middle, norm_gain[1], norm_bias[1])
    lifted = jnp.dot(second_norm.astype(jnp.bfloat16), upward, preferred_element_type=jnp.float32)
    active = jax.nn.gelu(lifted, approximate=False).astype(jnp.bfloat16)
    result = middle + jnp.dot(active, downward, preferred_element_type=jnp.float32)
    stored = (unit_one, scale_one, joined, logsum, attended, unit_two, scale_two, lifted, active)
    return (result, stored)


def contract_rows(left, right):
    return lax.dot_general(
        left, right, (((0,), (0,)), ((), ())), preferred_element_type=jnp.float32
    )


def contract_cols(left, right):
    return lax.dot_general(
        left, right, (((1,), (1,)), ((), ())), preferred_element_type=jnp.float32
    )


def feed_backward(incoming, stored, params):
    inward, outward, upward, downward, norm_gain, norm_bias = params
    unit_one, scale_one, joined, logsum, attended, unit_two, scale_two, lifted, active = stored
    branch = incoming.astype(jnp.bfloat16)
    down_part = contract_rows(active, branch)
    hidden_grad = contract_cols(branch, downward)
    lifted_grad = (hidden_grad * gelu_slope(lifted)).astype(jnp.bfloat16)
    second_in = (unit_two * norm_gain[1] + norm_bias[1]).astype(jnp.bfloat16)
    up_part = contract_rows(second_in, lifted_grad)
    normed_grad = contract_cols(lifted_grad, upward)
    through, gain_two, bias_two = norm_back(normed_grad, unit_two, scale_two, norm_gain[1])
    return (incoming + through, (up_part, down_part, gain_two, bias_two))


def attend_backward(middle_grad, stored, clip_ids, anchors, params):
    inward, outward, upward, downward, norm_gain, norm_bias = params
    unit_one, scale_one, joined, logsum, attended, unit_two, scale_two, lifted, active = stored
    length, model_width = attended.shape
    head_count = model_width // HEAD
    scaling = HEAD ** (-0.5)
    branch = middle_grad.astype(jnp.bfloat16)
    outward_part = contract_rows(attended, branch)
    attended_grad = (
        contract_cols(branch, outward).astype(jnp.bfloat16).reshape(length, head_count, HEAD)
    )
    heads_view = joined.reshape(length, 3, head_count, HEAD)
    queries = heads_view[:, 0]
    key_rows = heads_view[:, 1]
    values = heads_view[:, 2]
    key_grad = jnp.zeros((length, head_count, HEAD), jnp.float32)
    value_grad = jnp.zeros((length, head_count, HEAD), jnp.float32)
    block_rows = min(512, length)
    scores = masked_scores(queries, key_rows, clip_ids, clip_ids, anchors, scaling)
    weights = jnp.exp(scores - logsum[:, 0:block_rows, None])
    weight_grad = jnp.einsum(
        "qhd,khd->hqk", attended_grad, values, preferred_element_type=jnp.float32
    )
    score_grad = (
        weights * (weight_grad - jnp.sum(weights * weight_grad, -1, keepdims=True))
    ).astype(jnp.bfloat16)
    query_pieces = [
        scaling
        * jnp.einsum("hqk,khd->qhd", score_grad, key_rows, preferred_element_type=jnp.float32)
    ]
    key_grad = key_grad + scaling * jnp.einsum(
        "hqk,qhd->khd", score_grad, queries, preferred_element_type=jnp.float32
    )
    value_grad = value_grad + jnp.einsum(
        "hqk,qhd->khd",
        weights.astype(jnp.bfloat16),
        attended_grad,
        preferred_element_type=jnp.float32,
    )
    query_grad = jnp.concatenate(query_pieces, 0)
    joined_grad = (
        jnp.stack([query_grad, key_grad, value_grad], 1)
        .reshape(length, 3 * model_width)
        .astype(jnp.bfloat16)
    )
    first_in = (unit_one * norm_gain[0] + norm_bias[0]).astype(jnp.bfloat16)
    inward_part = contract_rows(first_in, joined_grad)
    normed_grad = contract_cols(joined_grad, inward)
    through, gain_one, bias_one = norm_back(normed_grad, unit_one, scale_one, norm_gain[0])
    return (middle_grad + through, (inward_part, outward_part, gain_one, bias_one))


def resting(function):

    def blank(*operands):
        return jax.tree.map(jnp.zeros_like, function(*operands))

    return blank


def take_slot(holder, buffer_slot):
    return jax.tree.map(
        lambda element: lax.dynamic_index_in_dim(element, buffer_slot, 0, False), holder
    )


def place_slot(holder, item, buffer_slot, working):

    def update(element, fresh):
        former = lax.dynamic_index_in_dim(element, buffer_slot, 0, False)
        return lax.dynamic_update_index_in_dim(
            element, jnp.where(working, fresh, former), buffer_slot, 0
        )

    return jax.tree.map(update, holder, item)


def per_device(
    inputs,
    clip_lengths,
    anchor_offsets,
    cotangent,
    inward_weight,
    outward_weight,
    up_weight,
    down_weight,
    norm_gain,
    norm_bias,
):
    params = (
        inward_weight[0],
        outward_weight[0],
        up_weight[0],
        down_weight[0],
        norm_gain[0],
        norm_bias[0],
    )
    stream = inputs[:, 0]
    cot_rows = cotangent[:, 0]
    lengths_all = clip_lengths[:, 0]
    offsets_all = anchor_offsets[:, 0]
    micro_count = stream.shape[0]
    length = stream.shape[1]
    section_index = lax.axis_index("section")
    section_count = lax.axis_size("section")
    leading = section_index == 0
    trailing = section_index == section_count - 1
    periods = micro_count + section_count - 1
    arriving = jnp.zeros_like(stream[0])
    produced = jnp.zeros_like(stream)
    archive = None
    for period in range(periods):
        micro_index = period - section_index
        working = (micro_index >= 0) & (micro_index < micro_count)
        buffer_slot = jnp.clip(micro_index, 0, micro_count - 1)
        source = jnp.where(leading, stream[min(period, micro_count - 1)], arriving)
        clip_ids, anchors = clip_marks(
            take_slot(lengths_all, buffer_slot), take_slot(offsets_all, buffer_slot), length
        )
        result, stored = lax.cond(
            working, forward_layer, resting(forward_layer), source, clip_ids, anchors, params
        )
        if archive is None:
            archive = jax.tree.map(
                lambda element: jnp.zeros((micro_count,) + element.shape, element.dtype), stored
            )
        archive = place_slot(archive, stored, buffer_slot, working)
        sending = result.astype(jnp.bfloat16)
        produced = place_slot(produced, sending, buffer_slot, working)
        if period < micro_count:
            arriving = shifted(sending, "section", 1)
    inward, outward, upward, downward, gains, biases = params
    up_sum = jnp.zeros(upward.shape, jnp.float32)
    down_sum = jnp.zeros(downward.shape, jnp.float32)
    gain_two = jnp.zeros(gains.shape[1:], jnp.float32)
    bias_two = jnp.zeros(biases.shape[1:], jnp.float32)
    inward_sum = jnp.zeros(inward.shape, jnp.float32)
    outward_sum = jnp.zeros(outward.shape, jnp.float32)
    gain_one = jnp.zeros(gains.shape[1:], jnp.float32)
    bias_one = jnp.zeros(biases.shape[1:], jnp.float32)
    upstream = jnp.zeros_like(stream[0])
    returned = jnp.zeros(stream.shape, jnp.float32)
    for period in range(periods):
        micro_index = micro_count - 1 - period + (section_count - 1 - section_index)
        working = (micro_index >= 0) & (micro_index < micro_count)
        buffer_slot = jnp.clip(micro_index, 0, micro_count - 1)
        incoming = jnp.where(trailing, take_slot(cot_rows, buffer_slot), upstream).astype(
            jnp.float32
        )
        clip_ids, anchors = clip_marks(
            take_slot(lengths_all, buffer_slot), take_slot(offsets_all, buffer_slot), length
        )
        stored = take_slot(archive, buffer_slot)
        middle_grad, feed_part = lax.cond(
            working, feed_backward, resting(feed_backward), incoming, stored, params
        )
        up_sum = up_sum + feed_part[0]
        down_sum = down_sum + feed_part[1]
        gain_two = gain_two + feed_part[2]
        bias_two = bias_two + feed_part[3]
        input_grad, attend_part = lax.cond(
            working,
            attend_backward,
            resting(attend_backward),
            middle_grad,
            stored,
            clip_ids,
            anchors,
            params,
        )
        inward_sum = inward_sum + attend_part[0]
        outward_sum = outward_sum + attend_part[1]
        gain_one = gain_one + attend_part[2]
        bias_one = bias_one + attend_part[3]
        returned = place_slot(returned, input_grad, buffer_slot, working)
        if period < periods - 1:
            upstream = shifted(input_grad.astype(jnp.bfloat16), "section", -1)
    inward_sum, outward_sum, up_sum, down_sum, gain_one, gain_two, bias_one, bias_two = (
        lax.psum_scatter(inward_sum, "dp", scatter_dimension=0, tiled=True),
        lax.psum_scatter(outward_sum, "dp", scatter_dimension=0, tiled=True),
        lax.psum_scatter(up_sum, "dp", scatter_dimension=0, tiled=True),
        lax.psum_scatter(down_sum, "dp", scatter_dimension=0, tiled=True),
        lax.psum_scatter(gain_one, "dp", scatter_dimension=0, tiled=True),
        lax.psum_scatter(gain_two, "dp", scatter_dimension=0, tiled=True),
        lax.psum_scatter(bias_one, "dp", scatter_dimension=0, tiled=True),
        lax.psum_scatter(bias_two, "dp", scatter_dimension=0, tiled=True),
    )
    layer_outputs = produced[None, :, None]
    input_grads = returned[None, :, None]
    gain_grad = jnp.stack([gain_one, gain_two])[None]
    bias_grad = jnp.stack([bias_one, bias_two])[None]
    return (
        layer_outputs,
        input_grads,
        inward_sum[None],
        outward_sum[None],
        up_sum[None],
        down_sum[None],
        gain_grad,
        bias_grad,
    )


def solution(mesh):
    return jax.shard_map(
        per_device,
        mesh=mesh,
        in_specs=(
            P(None, "dp", None, None),
            P(None, "dp", None),
            P(None, "dp", None),
            P(None, "dp", None, None),
            P("section", None, None),
            P("section", None, None),
            P("section", None, None),
            P("section", None, None),
            P("section", None, None),
            P("section", None, None),
        ),
        out_specs=(
            P("section", None, "dp", None, None),
            P("section", None, "dp", None, None),
            P("section", "dp", None),
            P("section", "dp", None),
            P("section", "dp", None),
            P("section", "dp", None),
            P("section", None, "dp"),
            P("section", None, "dp"),
        ),
        check_vma=False,
    )
```

profile of v0, /device:TPU:0, one launch (start us, length us, event | category | flops | bytes accessed | tf_op | source)
XLA Modules:
  0.0 726.9 jit_solution(12950612259555704241)
XLA Ops:
  10.7 34.3 %conditional.9 = (f32[256,768]{1,0:T(8,128)}, f32[256,1]{0,1:T(1,128)}, f32[12,256]{1,0:T(8,128)}, f32[256,768]{1,0:T(8,128)}, f32[256,1]{0,1:T(1,128)}, /*index...) conditional(s32[]{:T(128)} %convert_element_type.315, ...), branch_computations={%region_3.4_spmd, %region_4.11_spmd} | conditional | flops 3891787264 | bytes 78741024 | solution.py:238
  15.9 3.3 convolution_convert_fusion
  23.3 2.4 fusion.14
  29.1 10.0 %fusion.2 = (bf16[256,3072]{1,0:T(8,128)(2,1)}, f32[256,3072]{1,0:T(8,128)S(1)}) fusion(bf16[768,3072]{1,0:T(8,128)(2,1)S(1)} %bitcast.695, f32[256,768]{1,0:T(8,128)} %subtract_multiply_fusion, f32[768]{0:T(1024)S(1)} %copy-done.100, f32[768]{0:T(1024)S(1)} %copy-done.101), kind=kOutput, calls=%fused_computation.4 | convolution fusion | flops 1259667456 | bytes 10229760 | tf_op jit(solution)/shard_map/cond/branch_1_fun/dot_general | solution.py:86
  39.1 3.6 fusion.13
  45.0 2.2 collective-permute-start
  77.7 2.5 bitcast_dynamic-update-slice_fusion.8
  80.8 2.4 constant_dynamic-slice_fusion.25
  83.2 37.0 %conditional.10 = (f32[256,768]{1,0:T(8,128)}, f32[256,1]{0,1:T(1,128)}, f32[12,256]{1,0:T(8,128)S(1)}, f32[256,768]{1,0:T(8,128)}, f32[256,1]{0,1:T(1,128)}, /*...) conditional(s32[]{:T(128)} %convert_element_type.317, ...), branch_computations={%region_14.15_spmd, %region_15.22_spmd} | conditional | flops 3891787264 | bytes 78790264 | solution.py:238
  87.6 4.4 convolution_convert_fusion.1
  92.0 2.4 copy.112
  97.7 2.4 fusion.40
  103.6 10.4 %fusion.28 = (bf16[256,3072]{1,0:T(8,128)(2,1)}, f32[256,3072]{1,0:T(8,128)}) fusion(bf16[768,3072]{1,0:T(8,128)(2,1)S(1)} %bitcast.697, f32[256,768]{1,0:T(8,128)} %subtract_multiply_fusion.1, f32[768]{0:T(1024)S(1)} %copy-done.102, f32[768]{0:T(1024)S(1)} %copy-done.103), kind=kOutput, calls=%fused_computation.65 | convolution fusion | flops 1259667456 | bytes 10229760 | tf_op jit(solution)/shard_map/cond/branch_1_fun/dot_general | solution.py:86
  114.0 3.6 fusion.39
  124.4 3.8 bitcast_dynamic-update-slice_fusion.4
  128.2 2.9 constant_dynamic-slice_fusion.14
  137.0 2.5 bitcast_dynamic-update-slice_fusion.1
  145.8 2.7 bitcast_dynamic-update-slice_fusion.7
  149.1 2.3 constant_dynamic-slice_fusion.24
  151.5 9.5 %conditional.11 = (f32[256,768]{1,0:T(8,128)}, f32[256,1]{0,1:T(1,128)}, f32[12,256]{1,0:T(8,128)S(1)}, f32[256,768]{1,0:T(8,128)}, f32[256,1]{0,1:T(1,128)}, /*...) conditional(s32[]{:T(128)} %convert_element_type.319, ...), branch_computations={%region_25.26_spmd, %region_26.33_spmd} | conditional | flops 3891787264 | bytes 78790264 | solution.py:238
  162.8 3.5 bitcast_dynamic-update-slice_fusion.3
  172.5 5.5 conditional.12
  173.6 4.2 broadcast.1145
  179.9 3.5 bitcast_dynamic-update-slice_fusion.6
  183.4 2.9 conditional.13
  189.4 43.6 %collective-permute-done.2 = bf16[256,768]{1,0:T(8,128)(2,1)S(1)} collective-permute-done((bf16[256,768]{1,0:T(8,128)(2,1)S(1)}, bf16[256,768]{1,0:T(8,128)(2,1)S(1)}, u32[]{:S(2)}, u32[]{:S(2)}) %collective-permute-start.2) | collective-permute-done | bytes 393248 | tf_op jit(solution)/shard_map/ppermute | solution.py:15
  234.1 12.0 %conditional.14 = (f32[256,768]{1,0:T(8,128)S(1)}, f32[768,3072]{1,0:T(8,128)S(1)}, f32[3072,768]{1,0:T(8,128)S(1)}, f32[768]{0:T(1024)S(1)}, f32[768]{0:T(1024)S(1)}) conditional(s32[]{:T(128)} %convert_element_type.317, () %tuple.121, (f32[2,256,1]{1,2,0:T(1,128)}, s32[]{:T(128)}, f32[256,768]{1,0:T(8,128)S(1)}, bf16[3072,768]{1,0:T(8,128)(2,1)}, ...), branch_computations={%region_46.47_spmd, %region_47.52_spmd} | conditional | flops 4843239936 | bytes 82627768 | solution.py:272
  234.1 6.6 fusion.103
  246.7 3.1 copy-done.14
  249.7 2.9 copy-done.15
  252.6 18.7 %conditional.15 = (f32[256,768]{1,0:T(8,128)}, f32[768,2304]{1,0:T(8,128)S(1)}, f32[768,768]{1,0:T(8,128)}, f32[768]{0:T(1024)}, f32[768]{0:T(1024)}) conditional(s32[]{:T(128)} %convert_element_type.317, () %tuple.120, (f32[2,256,1]{1,2,0:T(1,128)}, s32[]{:T(128)}, s32[256]{0:T(256)}, pred[256]{0:T(512)(128)(4,1)}, ...), branch_computations={%region_52.53_spmd, %region_53.59_spmd} | conditional | flops 2932141568 | bytes 81351144 | solution.py:279
  252.6 2.4 constant_dynamic-slice_fusion.3
  274.4 10.9 %collective-permute-done.3 = bf16[256,768]{1,0:T(8,128)(2,1)S(1)} collective-permute-done((bf16[256,768]{1,0:T(8,128)(2,1)S(1)}, bf16[256,768]{1,0:T(8,128)(2,1)S(1)}, u32[]{:S(2)}, u32[]{:S(2)}) %collective-permute-start.3) | collective-permute-done | bytes 393248 | tf_op jit(solution)/shard_map/ppermute | solution.py:15
  286.4 12.2 %conditional.16 = (f32[256,768]{1,0:T(8,128)S(1)}, f32[768,3072]{1,0:T(8,128)S(1)}, f32[3072,768]{1,0:T(8,128)S(1)}, f32[768]{0:T(1024)S(1)}, f32[768]{0:T(1024)S(1)}) conditional(s32[]{:T(128)} %convert_element_type.315, () %tuple.125, (f32[2,256,1]{1,2,0:T(1,128)}, s32[]{:T(128)}, f32[256,768]{1,0:T(8,128)S(1)}, bf16[3072,768]{1,0:T(8,128)(2,1)}, ...), branch_computations={%region_59.60_spmd, %region_60.65_spmd} | conditional | flops 4843239936 | bytes 82627768 | solution.py:272
  286.8 6.4 fusion.154
  298.6 3.6 copy-done.16
  302.2 2.8 copy-done.17
  305.0 20.9 %conditional.17 = (f32[256,768]{1,0:T(8,128)}, f32[768,2304]{1,0:T(8,128)}, f32[768,768]{1,0:T(8,128)}, f32[768]{0:T(1024)}, f32[768]{0:T(1024)}) conditional(s32[]{:T(128)} %convert_element_type.315, () %tuple.124, (f32[2,256,1]{1,2,0:T(1,128)}, s32[]{:T(128)}, s32[256]{0:T(256)}, pred[256]{0:T(512)(128)(4,1)}, bf16[2,256,2304]{1,2,0:T(8,128)(2,1)}, ...), branch_computations={%region_65.66_spmd, %region_66.72_spmd} | conditional | flops 2932141568 | bytes 81351144 | solution.py:279
  305.1 2.4 constant_dynamic-slice_fusion.6
  317.0 4.0 fusion.193
  325.9 5.0 add_add_fusion.3
  330.9 11.3 %add_add_fusion.2 = f32[768,2304]{1,0:T(8,128)} fusion(f32[768,2304]{1,0:T(8,128)} %get-tuple-element.855, f32[768,2304]{1,0:T(8,128)} %copy-done.18, f32[768,2304]{1,0:T(8,128)} %copy-done.19), kind=kLoop, calls=%fused_computation.438 | loop fusion | flops 3538944 | bytes 28311552 | tf_op jit(solution)/shard_map/add | solution.py:289
  342.3 14.5 %add_add_fusion = f32[3072,768]{1,0:T(8,128)} fusion(f32[3072,768]{1,0:T(8,128)} %copy-done.17, f32[3072,768]{1,0:T(8,128)} %get-tuple-element.862, f32[3072,768]{1,0:T(8,128)} %copy-done.15), kind=kLoop, calls=%fused_computation.436 | loop fusion | flops 4718592 | bytes 37748736 | tf_op jit(solution)/shard_map/add | solution.py:276
  357.1 15.2 %add_add_fusion.1 = f32[768,3072]{1,0:T(8,128)} fusion(f32[768,3072]{1,0:T(8,128)} %copy-done.16, f32[768,3072]{1,0:T(8,128)} %copy-done.13, f32[768,3072]{1,0:T(8,128)} %copy-done.14), kind=kLoop, calls=%fused_computation.437 | loop fusion | flops 4718592 | bytes 37748736 | tf_op jit(solution)/shard_map/add | solution.py:275
  378.9 59.5 %all-reduce.4 = (f32[768]{0:T(1024)S(1)}, f32[768]{0:T(1024)S(1)}, f32[768]{0:T(1024)S(1)}, f32[768]{0:T(1024)S(1)}) all-reduce(f32[768]{0:T(1024)S(1)} %add_add_fusion.6, f32[768]{0:T(1024)S(1)} %add_add_fusion.7, f32[768]{0:T(1024)S(1)} %add_add_fusion.4, f32[768]{0:T(1024)S(1)} %add_add_fusion.5), channel_id=7, replica_groups=mesh['section'=2,'dp'=16] {'dp'}, use_global_device_ids=true, to_apply=%region_77.78.clone | all-reduce | flops 3072 | bytes 24576
  441.1 47.2 %reduce-scatter.5.cloned.1.call-done = f32[48,2304]{1,0:T(8,128)} async-done(((f32[768,2304]{1,0:T(8,128)}), f32[48,2304]{1,0:T(8,128)}) %reduce-scatter.5.cloned.1.call-update) | async-done | bytes 442384 | tf_op jit(solution)/shard_map/reduce_scatter | solution.py:297
  488.4 115.6 %reduce-scatter.11.cloned.1.call-done = f32[192,768]{1,0:T(8,128)} async-done(((f32[3072,768]{1,0:T(8,128)}), f32[192,768]{1,0:T(8,128)}) %reduce-scatter.11.cloned.1.call-update) | async-done | bytes 589840 | tf_op jit(solution)/shard_map/reduce_scatter | solution.py:300
  604.0 116.2 %reduce-scatter.9.cloned.1.call-done = f32[48,3072]{1,0:T(8,128)} async-done(((f32[768,3072]{1,0:T(8,128)}), f32[48,3072]{1,0:T(8,128)}) %reduce-scatter.9.cloned.1.call-update) | async-done | bytes 589840 | tf_op jit(solution)/shard_map/reduce_scatter | solution.py:299
  (440 shorter events, 161.3 us)
Async XLA Ops:
  7.2 434.0 %reduce-scatter.7.cloned.1.call-start = ((), (), s32[]{:S(2)}) async-start(), calls=%async_computation.5 | async-start | bytes 2506752 | tf_op jit(solution)/shard_map/reduce_scatter | solution.py:298
  22.6 6.5 slice-start.2
  23.3 5.8 slice-start.3
  27.2 12.0 %slice-start.8 = ((s8[4718592]{0:T(1024)(128)(4,1)}), s8[4194304]{0:T(1024)(128)(4,1)S(1)}, s32[]{:S(2)}) async-start(s8[4718592]{0:T(1024)(128)(4,1)} %bitcast.706), calls=%async_computation.16 | async-start | bytes 8388608 | tf_op jit(solution)/shard_map/cond
  29.1 10.1 %slice-start.9 = ((s8[4718592]{0:T(1024)(128)(4,1)}), s8[524288]{0:T(1024)(128)(4,1)S(1)}, s32[]{:S(2)}) async-start(s8[4718592]{0:T(1024)(128)(4,1)} %bitcast.706), calls=%async_computation.17 | async-start | bytes 1048576 | tf_op jit(solution)/shard_map/cond
  45.0 12.5 %copy-start.24 = (f32[256,3072]{1,0:T(8,128)}, f32[256,3072]{1,0:T(8,128)S(1)}, u32[]{:S(2)}) copy-start(f32[256,3072]{1,0:T(8,128)S(1)} %get-tuple-element.832) | copy-start | bytes 9437188
  45.0 38.2 %collective-permute-start = (bf16[256,768]{1,0:T(8,128)(2,1)}, bf16[256,768]{1,0:T(8,128)(2,1)}, u32[]{:S(2)}, u32[]{:S(2)}) collective-permute-start(bf16[256,768]{1,0:T(8,128)(2,1)} %get-tuple-element.817), channel_id=1, source_target_pairs={{0,16},{1,17},{2,18},{3,19},{4,20},{5,21},{6,22},{7,23},{8,24},{9,... | collective-permute-start | bytes 1179656 | tf_op jit(solution)/shard_map/ppermute | solution.py:15
  50.1 24.4 %copy-start.34 = (bf16[2,256,768]{2,1,0:T(8,128)(2,1)}, bf16[2,256,768]{2,1,0:T(8,128)(2,1)S(1)}, u32[]{:S(2)}) copy-start(bf16[2,256,768]{2,1,0:T(8,128)(2,1)S(1)} %bitcast_dynamic-update-slice_fusion.23) | copy-start | bytes 2359300
  76.1 7.1 copy-start
  76.1 7.1 copy-start.61
  76.1 7.1 copy-start.62
  97.0 6.6 slice-start.4
  97.7 5.9 slice-start.5
  101.7 12.3 %slice-start.10 = ((s8[4718592]{0:T(1024)(128)(4,1)}), s8[4194304]{0:T(1024)(128)(4,1)S(1)}, s32[]{:S(2)}) async-start(s8[4718592]{0:T(1024)(128)(4,1)} %bitcast.708), calls=%async_computation.18 | async-start | bytes 8388608 | tf_op jit(solution)/shard_map/cond
  103.6 10.4 %slice-start.11 = ((s8[4718592]{0:T(1024)(128)(4,1)}), s8[524288]{0:T(1024)(128)(4,1)S(1)}, s32[]{:S(2)}) async-start(s8[4718592]{0:T(1024)(128)(4,1)} %bitcast.708), calls=%async_computation.19 | async-start | bytes 1048576 | tf_op jit(solution)/shard_map/cond
  122.8 28.6 %collective-permute-start.1 = (bf16[256,768]{1,0:T(8,128)(2,1)}, bf16[256,768]{1,0:T(8,128)(2,1)S(1)}, u32[]{:S(2)}, u32[]{:S(2)}) collective-permute-start(bf16[256,768]{1,0:T(8,128)(2,1)} %get-tuple-element.818), channel_id=1, source_target_pairs={{0,16},{1,17},{2,18},{3,19},{4,20},{5,21},{6,22},{7,23},{8,24},{9,... | collective-permute-start | bytes 1179656 | tf_op jit(solution)/shard_map/ppermute | solution.py:15
  124.4 6.7 copy-start.48
  124.4 12.6 %slice-start = ((s8[6291456]{0:T(1024)(128)(4,1)}), s8[4194304]{0:T(1024)(128)(4,1)S(1)}, s32[]{:S(2)}) async-start(s8[6291456]{0:T(1024)(128)(4,1)} %bitcast.627), calls=%async_computation.8 | async-start | bytes 8388608
  131.1 5.9 slice-start.1
  139.5 5.6 copy-start.81
  139.5 5.6 copy-start.109
  139.5 6.2 copy-start.40
  143.0 8.4 %copy-start.41 = (bf16[256,768]{1,0:T(8,128)(2,1)S(1)}, bf16[256,768]{1,0:T(8,128)(2,1)}, u32[]{:S(2)}) copy-start(bf16[256,768]{1,0:T(8,128)(2,1)} %slice_bitcast_fusion.42) | copy-start | bytes 1179652
  143.1 8.4 %copy-start.117 = (bf16[1,768,2304]{2,1,0:T(8,128)(2,1)S(1)}, bf16[1,768,2304]{2,1,0:T(8,128)(2,1)}, u32[]{:S(2)}) copy-start(bf16[1,768,2304]{2,1,0:T(8,128)(2,1)} %param.32) | copy-start | bytes 10616836
  143.9 7.5 %copy-start.74 = (f32[2,256,1]{1,2,0:T(1,128)}, f32[2,256,1]{1,2,0:T(1,128)S(1)}, u32[]{:S(2)}) copy-start(f32[2,256,1]{1,2,0:T(1,128)S(1)} %constant_dynamic-update-slice_fusion.4) | copy-start | bytes 6148
  144.5 7.0 copy-start.57
  145.8 5.7 copy-start.82
  162.8 5.7 copy-start.26
  162.8 6.8 copy-start.116
  178.0 5.4 copy-start.13
  178.0 5.4 copy-start.88
  186.3 47.8 %copy-start.18 = (f32[768,2304]{1,0:T(8,128)}, f32[768,2304]{1,0:T(8,128)S(1)}, u32[]{:S(2)}) copy-start(f32[768,2304]{1,0:T(8,128)S(1)} %get-tuple-element.853) | copy-start | bytes 21233668
  186.3 47.8 %copy-start.30 = (f32[768,768]{1,0:T(8,128)}, f32[768,768]{1,0:T(8,128)S(1)}, u32[]{:S(2)}) copy-start(f32[768,768]{1,0:T(8,128)S(1)} %get-tuple-element.856) | copy-start | bytes 7077892
  188.1 44.9 %collective-permute-start.2 = (bf16[256,768]{1,0:T(8,128)(2,1)S(1)}, bf16[256,768]{1,0:T(8,128)(2,1)S(1)}, u32[]{:S(2)}, u32[]{:S(2)}) collective-permute-start(bf16[256,768]{1,0:T(8,128)(2,1)S(1)} %convert_element_type.323), channel_id=1, source_target_pairs={{16,0},{17,1},{18,2},{19,3},{20,4},{21,5},{22,6},{23,7},{24,8},{25... | collective-permute-start | bytes 1179656 | tf_op jit(solution)/shard_map/ppermute | solution.py:15
  234.1 6.6 copy-start.7
  234.1 6.6 copy-start.114
  246.1 6.5 copy-start.15
  271.3 15.0 %copy-start.19 = (f32[768,2304]{1,0:T(8,128)}, f32[768,2304]{1,0:T(8,128)S(1)}, u32[]{:S(2)}) copy-start(f32[768,2304]{1,0:T(8,128)S(1)} %get-tuple-element.854) | copy-start | bytes 21233668
  273.1 12.2 %collective-permute-start.3 = (bf16[256,768]{1,0:T(8,128)(2,1)S(1)}, bf16[256,768]{1,0:T(8,128)(2,1)S(1)}, u32[]{:S(2)}, u32[]{:S(2)}) collective-permute-start(bf16[256,768]{1,0:T(8,128)(2,1)S(1)} %convert_element_type.325), channel_id=1, source_target_pairs={{16,0},{17,1},{18,2},{19,3},{20,4},{21,5},{22,6},{23,7},{24,8},{25... | collective-permute-start | bytes 1179656 | tf_op jit(solution)/shard_map/ppermute | solution.py:15
  286.8 6.4 copy-start.8
  286.8 6.4 copy-start.115
  298.6 6.4 copy-start.17
  298.6 6.4 copy-start.96
  298.6 6.4 copy-start.98
  330.9 157.5 %reduce-scatter.5.cloned.1.call-start = ((), (), s32[]{:S(2)}) async-start(), calls=%async_computation.4 | async-start | bytes 7520256 | tf_op jit(solution)/shard_map/reduce_scatter | solution.py:297
  342.3 261.7 %reduce-scatter.11.cloned.1.call-start = ((), (), s32[]{:S(2)}) async-start(), calls=%async_computation.7 | async-start | bytes 10027008 | tf_op jit(solution)/shard_map/reduce_scatter | solution.py:300
  356.8 363.4 %reduce-scatter.9.cloned.1.call-start = ((), (), s32[]{:S(2)}) async-start(), calls=%async_computation.6 | async-start | bytes 10027008 | tf_op jit(solution)/shard_map/reduce_scatter | solution.py:299
  441.1 279.1 %copy-start.50 = (f32[1,2,1,256,768]{4,3,2,1,0:T(8,128)}, f32[1,2,1,256,768]{4,3,2,1,0:T(8,128)S(1)}, u32[]{:S(2)}) copy-start(f32[1,2,1,256,768]{4,3,2,1,0:T(8,128)S(1)} %bitcast_dynamic-update-slice_fusion.9) | copy-start | bytes 4718596
  (79 other events, 197.6 us)
Sparse Core Ops, SparseCore 0:
  331.0 63.1 reduce-scatter.6
  399.3 89.0 reduce-scatter.4
  493.1 110.8 reduce-scatter.10
  609.1 111.0 reduce-scatter.8
where the time goes:
time: 737 us; the launch traced here: 727 us
  waiting for transfers between devices  334 us (45%)
  other arithmetic  127 us (17%)
  local copies, waits for them, and re-layouts  91.3 us (12%)
  matrix products  91 us (12%)
  blocking collectives  59.5 us (8%)
  between operations  15.6 us (2%)
    reduce_scatter x1, waiting for transfers between devices, per_device(): lax.psum_scatter(up_sum, 'dp', scatter_dimension=0, tiled=True)  116 us
    reduce_scatter x1, waiting for transfers between devices, per_device(): lax.psum_scatter(down_sum, 'dp', scatter_dimension=0, tiled=True)  116 us
    unnamed x1, blocking collectives  59.5 us
    ppermute x4, waiting for transfers between devices, shifted(): return lax.ppermute(x, axis, pairs)  54.6 us
    reduce_scatter x1, waiting for transfers between devices, per_device(): lax.psum_scatter(inward_sum, 'dp', scatter_dimension=0, tiled=True)  47.2 us
    dynamic_update_slice x31, other arithmetic, update(): lax.dynamic_update_index_in_dim(element, jnp.where(working, fresh, former...  42.5 us
    unnamed x163, local copies, waits for them, and re-layouts  26.4 us
    dot_general x8, matrix products, contract_cols(): lax.dot_general(left, right, (((1,), (1,)), ((), ())), preferred_element_...  22.4 us
  transfers between devices with their start and end apart: 8, of which 5 were waited for; matrix products, arithmetic and copies ran while one was open for 14% of the time, Pallas kernels for 0%

commit v1 on v0

--- a/solution.py
+++ b/solution.py
@@ -1,12 +1,638 @@
+import functools
+import types
+
 import jax
 import jax.numpy as jnp
 from jax import lax
+from jax.experimental import pallas as pl
+from jax.experimental.pallas import tpu as pltpu
 from jax.sharding import PartitionSpec as P
 
 HEAD = 64
-
-
 EPSILON = 1e-06
+MESH = pl.DeviceIdType.MESH
+WIDE = jnp.float32
+SLIM = jnp.bfloat16
+VMEM_BYTES = 67043328
+
+UNITS = 12
+BLOCK = 48
+
+
+def times(left, right):
+    return jnp.dot(left, right, preferred_element_type=WIDE)
+
+
+def times_turned(left, right):
+    return lax.dot_general(left, right, (((1,), (1,)), ((), ())), preferred_element_type=WIDE)
+
+
+def unit_rows(values):
+    centred = values - jnp.mean(values, -1, keepdims=True)
+    inverse = lax.rsqrt(jnp.mean(centred * centred, -1, keepdims=True) + EPSILON)
+    return centred * inverse, inverse
+
+
+def norm_rows_bf16(r, values, which):
+    unit, _ = unit_rows(values)
+    return (unit * r.gain[0, which : which + 1, :] + r.bias[0, which : which + 1, :]).astype(SLIM)
+
+
+def norm_backward(r, values, norm_grad, which):
+    unit, inverse = unit_rows(values)
+    width = values.shape[1]
+    r.sums[which] += jnp.sum((norm_grad * unit).reshape(-1, 8, width), 0)
+    r.sums[2 + which] += jnp.sum(norm_grad.reshape(-1, 8, width), 0)
+    inner = norm_grad * r.gain[0, which : which + 1, :]
+    return inverse * (
+        inner
+        - jnp.mean(inner, -1, keepdims=True)
+        - unit * jnp.mean(inner * unit, -1, keepdims=True)
+    )
+
+
+def head_lanes():
+    lane = lax.broadcasted_iota(jnp.int32, (1, 2 * HEAD), 1)
+    first = jnp.where(lane < HEAD, 1.0, 0.0).astype(WIDE)
+    return first, 1.0 - first
+
+
+def mask_bias(r, micro):
+    length = r.bias_mask.shape[0]
+
+    def marks(positions):
+        end = jnp.int32(0)
+        ids = jnp.zeros(positions.shape, jnp.int32)
+        anchors = jnp.zeros(positions.shape, jnp.int32)
+        for clip in range(r.lengths.shape[2]):
+            size = r.lengths[micro, 0, clip]
+            anchor = end + lax.rem(r.offsets[micro, 0, clip], size)
+            end = end + size
+            ids = ids + jnp.where(positions >= end, 1, 0)
+            anchors = anchors + jnp.where(positions == anchor, 1, 0)
+        return ids, anchors
+
+    key_ids, anchors = marks(lax.broadcasted_iota(jnp.int32, (length, 1), 0))
+    query_ids, _ = marks(lax.broadcasted_iota(jnp.int32, (1, length), 1))
+    seen = (key_ids == query_ids) | (jnp.broadcast_to(anchors, (length, length)) > 0)
+    r.bias_mask[...] = jnp.where(seen, 0.0, -1000000000.0).astype(WIDE)
+
+
+def place(r, slab, tokens):
+    for line in range(8):
+        z, y = line // 2, line % 2
+        rows = pl.ds(y * 192 + z * BLOCK, BLOCK)
+        own = pl.ds(pl.multiple_of(2 * BLOCK * line + r.c * BLOCK, 16), BLOCK)
+        other = pl.ds(pl.multiple_of(2 * BLOCK * line + (1 - r.c) * BLOCK, 16), BLOCK)
+        r.acts[slab, rows, tokens] = r.turned[own, :]
+        r.acts_out[slab, rows, :] = r.turned[other, :]
+
+
+def forward(r, micro, tok, first):
+    length, width = r.normed.shape
+    tokens = pl.ds(tok, length)
+    mask_bias(r, micro)
+    r.normed[...] = norm_rows_bf16(r, r.stream[micro].astype(WIDE), 0)
+
+    @pl.when(first)
+    def _():
+        r.load_inward.wait()
+
+    for part in range(3):
+        r.grads[6 + part, tokens, :] = times(
+            r.normed[...], r.inward[:, part * width : (part + 1) * width]
+        ).astype(SLIM)
+
+    @pl.when(micro > 0)
+    def _():
+        r.share_acts(0).wait_send()
+
+    r.turned[...] = r.normed[...].T
+    place(r, 6, tokens)
+    one, two = (lanes.astype(SLIM) for lanes in head_lanes())
+    for pair in range(width // (2 * HEAD)):
+        cols = pl.ds(pair * 2 * HEAD, 2 * HEAD)
+        queries = r.grads[6, tokens, cols] * jnp.asarray(HEAD**-0.5, SLIM)
+        keys = r.grads[7, tokens, cols]
+        values_turned = r.grads[8, tokens, cols].T
+        scores = times_turned(jnp.concatenate([keys * one, keys * two], 0), queries)
+        pieces = []
+        for head in range(2):
+            masked = scores[length * head : length * (head + 1)] + r.bias_mask[...]
+            raised = jnp.exp(masked - jnp.max(masked, 0, keepdims=True))
+            weights = (raised * (1.0 / jnp.sum(raised, 0, keepdims=True))).astype(SLIM)
+            r.weights[micro, 2 * pair + head] = weights
+            pieces.append(times(values_turned[HEAD * head : HEAD * (head + 1)], weights).astype(SLIM))
+        attended_turned = jnp.concatenate(pieces, 0)
+        r.turned[cols, :] = attended_turned
+        r.held[:, cols] = attended_turned.T
+    place(r, 5, tokens)
+
+    @pl.when(first)
+    def _():
+        r.load_outward.wait()
+        r.load_up.wait()
+        r.load_down.wait()
+
+    r.middle[micro] = r.stream[micro].astype(WIDE) + times(r.held[...], r.outward[...])
+    r.normed[...] = norm_rows_bf16(r, r.middle[micro], 1)
+    r.turned[...] = r.normed[...].T
+    place(r, 4, tokens)
+    r.total[...] = r.middle[micro]
+    for part in range(4):
+        cols = slice(part * width, (part + 1) * width)
+        lifted = times(r.normed[...], r.up[:, cols])
+        cumulative = 0.5 * (1.0 + lax.erf(lifted * 0.7071067811865476))
+        density = jnp.exp(-0.5 * lifted * lifted) * 0.3989422804014327
+        r.grads[1 + part, tokens, :] = (cumulative + lifted * density).astype(SLIM)
+        active = (lifted * cumulative).astype(SLIM)
+        r.total[...] += times(active, r.down[cols, :])
+        r.turned[...] = active.T
+        for y in range(2):
+            for piece in range(4):
+                rows = pl.ds(y * 192 + part * BLOCK, BLOCK)
+                start = 384 * y + BLOCK * piece
+                own = pl.ds(pl.multiple_of(start + r.c * 192, 16), BLOCK)
+                other = pl.ds(pl.multiple_of(start + (1 - r.c) * 192, 16), BLOCK)
+                r.acts[piece, rows, tokens] = r.turned[own, :]
+                r.acts_out[piece, rows, :] = r.turned[other, :]
+    r.result[micro] = r.total[...].astype(SLIM)
+
+
+def backward(r, micro, tok):
+    length, width = r.normed.shape
+    tokens = pl.ds(tok, length)
+    r.total[...] = jnp.zeros((length, width), WIDE)
+    for part in range(4):
+        cols = slice(part * width, (part + 1) * width)
+        hidden = times_turned(r.grads[0, tokens, :], r.down[cols, :])
+        lifted_grad = (hidden * r.grads[1 + part, tokens, :].astype(WIDE)).astype(SLIM)
+        r.grads[1 + part, tokens, :] = lifted_grad
+        r.total[...] += times_turned(lifted_grad, r.up[:, cols])
+    middle_grad = r.grads[0, tokens, :].astype(WIDE) + norm_backward(
+        r, r.middle[micro], r.total[...], 1
+    )
+    r.middle[micro] = middle_grad
+    r.grads[5, tokens, :] = middle_grad.astype(SLIM)
+    r.held[...] = times_turned(r.grads[5, tokens, :], r.outward[...]).astype(SLIM)
+    first, second = head_lanes()
+    one, two = first.astype(SLIM), second.astype(SLIM)
+    scaling = HEAD**-0.5
+    for pair in range(width // (2 * HEAD)):
+        cols = pl.ds(pair * 2 * HEAD, 2 * HEAD)
+        queries = r.grads[6, tokens, cols] * jnp.asarray(scaling, SLIM)
+        values = r.grads[8, tokens, cols]
+        keys_turned = r.grads[7, tokens, cols].T
+        incoming = r.held[:, cols]
+        weight_grads = times_turned(jnp.concatenate([values * one, values * two], 0), incoming)
+        score_grads, query_grads, weights = [], [], []
+        for head in range(2):
+            kept = r.weights[micro, 2 * pair + head]
+            wide = kept.astype(WIDE)
+            own = weight_grads[length * head : length * (head + 1)]
+            score_grad = (wide * (own - jnp.sum(wide * own, 0, keepdims=True))).astype(SLIM)
+            score_grads.append(score_grad)
+            weights.append(kept)
+            query_grads.append(
+                (times(keys_turned[HEAD * head : HEAD * (head + 1)], score_grad) * scaling).astype(SLIM)
+            )
+        key_grad = times(jnp.concatenate(score_grads, 0), queries)
+        value_grad = times(jnp.concatenate(weights, 0), incoming)
+        r.grads[6, tokens, cols] = jnp.concatenate(query_grads, 0).T
+        r.grads[7, tokens, cols] = (key_grad[:length] * first + key_grad[length:] * second).astype(SLIM)
+        r.grads[8, tokens, cols] = (value_grad[:length] * first + value_grad[length:] * second).astype(SLIM)
+    norm_grad = times_turned(r.grads[6, tokens, :], r.inward[:, 0:width])
+    for part in range(1, 3):
+        norm_grad += times_turned(r.grads[6 + part, tokens, :], r.inward[:, part * width : (part + 1) * width])
+    r.total[...] = norm_grad
+    input_grad = r.middle[micro] + norm_backward(r, r.stream[micro].astype(WIDE), r.total[...], 0)
+    r.middle[micro] = input_grad
+    r.passed[micro] = input_grad.astype(SLIM)
+
+
+NAMES = (
+    "x_in", "cot_in", "inward_in", "outward_in", "up_in", "down_in", "gain", "bias", "lengths", "offsets",
+    "out_result", "out_grad", "out_weights", "out_norms",
+    "stream", "inward", "outward", "up", "down", "grads", "acts", "acts_out", "weights", "middle", "normed", "held",
+    "turned", "total", "result", "passed", "sums", "bias_mask",
+    "partial", "y_in", "z_in", "staged", "norms",
+    "load_sem", "source_sem", "store_sem", "unit_sem",
+    "relay_send", "relay_recv", "acts_send", "acts_recv", "branch_send", "branch_recv", "grads_send", "grads_recv",
+    "y_send", "y_recv", "z_send", "z_recv", "norm_send", "norm_recv",
+)
+
+
+def step_kernel(*refs):
+    r = types.SimpleNamespace(**dict(zip(NAMES, refs)))
+    section, dp = lax.axis_index("section"), lax.axis_index("dp")
+    c, y, z = lax.rem(dp, 2), lax.rem(lax.div(dp, 2), 2), lax.div(dp, 4)
+    r.c = c
+    length = r.normed.shape[0]
+    leading = section == 0
+    pair_dp, y_dp = dp + 1 - 2 * c, dp + 2 - 4 * y
+
+    def slot_of(core, micro):
+        return pl.ds(pl.multiple_of((core * 2 + micro) * length, length), length)
+
+    def remote(src, dst, send, recv, to_section, to_dp):
+        return pltpu.make_async_remote_copy(
+            src_ref=src, dst_ref=dst, send_sem=send, recv_sem=recv,
+            device_id=(to_section, to_dp), device_id_type=MESH,
+        )
+
+    def local(src, dst, sem):
+        return pltpu.make_async_copy(src, dst, sem)
+
+    r.load_inward = local(r.inward_in.at[0], r.inward, r.load_sem.at[0])
+    r.load_outward = local(r.outward_in.at[0], r.outward, r.load_sem.at[1])
+    r.load_up = local(r.up_in.at[0], r.up, r.load_sem.at[2])
+    r.load_down = local(r.down_in.at[0], r.down, r.load_sem.at[3])
+
+    def load_x(micro):
+        return local(r.x_in.at[micro, 0], r.stream.at[micro], r.source_sem.at[micro])
+
+    def load_cot(micro):
+        return local(r.cot_in.at[micro, 0], r.grads.at[0, slot_of(c, micro)], r.source_sem.at[micro])
+
+    def relay_up(micro):
+        return remote(r.result.at[micro], r.stream.at[micro], r.relay_send.at[micro], r.relay_recv.at[micro], 1 - section, dp)
+
+    def relay_back(micro):
+        return remote(
+            r.passed.at[micro], r.grads.at[0, slot_of(c, micro)], r.relay_send.at[micro], r.relay_recv.at[micro], 1 - section, dp
+        )
+
+    def share_acts(micro, core=c):
+        return remote(
+            r.acts_out, r.acts.at[:, :, slot_of(core, micro)], r.acts_send.at[micro], r.acts_recv.at[micro], section, pair_dp
+        )
+
+    def share_branch(micro, core=c):
+        rows = slot_of(core, micro)
+        return remote(r.grads.at[0, rows], r.grads.at[0, rows], r.branch_send.at[micro], r.branch_recv.at[micro], section, pair_dp)
+
+    def share_grads(micro, core=c):
+        rows = slot_of(core, micro)
+        return remote(
+            r.grads.at[1:9, rows], r.grads.at[1:9, rows], r.grads_send.at[micro], r.grads_recv.at[micro], section, pair_dp
+        )
+
+    r.share_acts = share_acts
+
+    def store_result(micro):
+        return local(r.result.at[micro], r.out_result.at[micro], r.store_sem.at[0, micro])
+
+    def store_grad(micro):
+        return local(r.middle.at[micro], r.out_grad.at[micro], r.store_sem.at[1, micro])
+
+    def to_y(unit):
+        return remote(r.partial.at[unit, 0:192], r.y_in.at[unit], r.y_send.at[unit], r.y_recv.at[unit], section, y_dp)
+
+    def kept(place):
+        return pl.ds(192 + BLOCK * place, BLOCK)
+
+    def to_right(unit, place):
+        return remote(
+            r.partial.at[unit, kept(place)], r.z_in.at[unit, place + 1],
+            r.z_send.at[unit, place - 1], r.z_recv.at[unit, place + 1], section, dp + 4,
+        )
+
+    def to_left(unit, place):
+        return remote(
+            r.partial.at[unit, kept(place)], r.z_in.at[unit, place],
+            r.z_send.at[unit, place], r.z_recv.at[unit, place], section, dp - 4,
+        )
+
+    def store_unit(unit):
+        return local(r.staged.at[unit], r.out_weights.at[unit], r.unit_sem.at[unit])
+
+    r.load_inward.start()
+
+    @pl.when(leading)
+    def _():
+        load_x(0).start()
+        load_x(1).start()
+
+    @pl.when(jnp.logical_not(leading))
+    def _():
+        load_cot(0).start()
+        load_cot(1).start()
+
+    r.load_outward.start()
+    r.load_up.start()
+    r.load_down.start()
+    r.sums[...] = jnp.zeros_like(r.sums)
+
+    barrier = pltpu.get_barrier_semaphore()
+    peers = [(1 - section, dp), (section, pair_dp), (section, y_dp)]
+    peers += [(section, lax.rem(dp + 4 * hop, 16)) for hop in (1, 2, 3)]
+    for peer in peers:
+        pl.semaphore_signal(barrier, inc=1, device_id=peer, device_id_type=MESH)
+    pl.semaphore_wait(barrier, len(peers))
+
+    def arrive(micro):
+        relay_back(micro).wait_recv()
+        share_branch(micro).start()
+
+    def weight_unit(unit):
+        slab = jnp.minimum(unit, 4) + jnp.where(unit >= 8, 1, 0) + jnp.where(unit >= 9, 1, 0)
+        column = jnp.maximum(unit - 3, 0)
+        other = pl.ds(pl.multiple_of((1 - y) * 192, 64), 192)
+        own = pl.ds(pl.multiple_of(y * 192, 64), 192)
+        r.partial[unit, 0:192, :] = times(r.acts[slab, other, :], r.grads[column]).astype(SLIM)
+        to_y(unit).start()
+        r.partial[unit, 192:384, :] = times(r.acts[slab, own, :], r.grads[column]).astype(SLIM)
+
+    def weight_units(low, high):
+        def body(unit, carry):
+            weight_unit(unit)
+            return carry
+
+        lax.fori_loop(low, high, body, 0)
+
+    def slot(t, carry):
+        trailing = jnp.logical_not(leading)
+        half = lax.div(t, 2)
+        is_forward = (leading & (t < 2)) | (trailing & ((t == 1) | (t == 3)))
+        is_backward = (leading & ((t == 3) | (t == 5))) | (trailing & ((t == 2) | (t == 4)))
+        is_weights = (leading & (t == 4)) | (trailing & (t == 5))
+
+        @pl.when(trailing & (t == 0))
+        def _():
+            for micro in range(2):
+                load_cot(micro).wait()
+                share_branch(micro).start()
+
+        @pl.when(is_forward)
+        def _():
+            micro = jnp.where(leading, jnp.minimum(t, 1), jnp.minimum(half, 1))
+
+            @pl.when(leading)
+            def _():
+                load_x(micro).wait()
+
+            @pl.when(trailing)
+            def _():
+                relay_up(micro).wait_recv()
+
+            forward(r, micro, pl.multiple_of((c * 2 + micro) * length, length), t == section)
+
+            @pl.when(leading)
+            def _():
+                relay_up(micro).start()
+
+            share_acts(micro).start()
+            store_result(micro).start()
+
+        @pl.when(leading & (t == 3))
+        def _():
+            arrive(0)
+
+        @pl.when(is_backward)
+        def _():
+            micro = jnp.clip(half - 1, 0, 1)
+            backward(r, micro, pl.multiple_of((c * 2 + micro) * length, length))
+
+            @pl.when(trailing)
+            def _():
+                relay_back(micro).start()
+
+            share_grads(micro).start()
+            store_grad(micro).start()
+
+        @pl.when(leading & (t == 4))
+        def _():
+            arrive(1)
+
+        @pl.when(is_weights)
+        def _():
+            for micro in range(2):
+                share_branch(micro, 1 - c).wait_recv()
+                share_acts(micro, 1 - c).wait_recv()
+            weight_units(0, 4)
+
+        return carry
+
+    lax.fori_loop(0, 6, slot, 0)
+
+    def norm_copy(src, dst, index, to_dp):
+        return remote(r.norms.at[src], r.norms.at[dst], r.norm_send.at[index], r.norm_recv.at[index], section, to_dp)
+
+    def norm_to_pair():
+        return norm_copy(0, 1, 0, pair_dp)
+
+    def norm_to_y():
+        return norm_copy(2, 3, 1, y_dp)
+
+    def norm_to_z(hop):
+        return norm_copy(4, 4 + hop, 1 + hop, lax.rem(dp + 4 * hop, 16))
+
+    r.norms[0] = jnp.concatenate([jnp.sum(r.sums[...], 1), jnp.zeros((4, r.sums.shape[2]), WIDE)], 0)
+    norm_to_pair().start()
+    norm_to_pair().wait_recv()
+    r.norms[2] = r.norms[0] + r.norms[1]
+    norm_to_y().start()
+    for micro in range(2):
+        share_grads(micro, 1 - c).wait_recv()
+    weight_units(4, UNITS)
+
+    def sum_y(unit):
+        to_y(unit).wait_recv()
+        r.partial[unit, 192:384, :] = (
+            r.partial[unit, 192:384, :].astype(WIDE) + r.y_in[unit].astype(WIDE)
+        ).astype(SLIM)
+
+    def arrived(unit, index):
+        remote(
+            r.partial.at[unit, kept(0)], r.z_in.at[unit, index], r.z_send.at[unit, 0], r.z_recv.at[unit, index], section, dp
+        ).wait_recv()
+        return r.z_in[unit, index].astype(WIDE)
+
+    def go_right(unit, here):
+        for place in range(3, here, -1):
+            if here > 0:
+                value = r.partial[unit, kept(place), :].astype(WIDE) + arrived(unit, place + 1)
+                r.partial[unit, kept(place), :] = value.astype(SLIM)
+            to_right(unit, place).start()
+
+    def go_left(unit, here):
+        for place in range(here):
+            if here < 3:
+                value = r.partial[unit, kept(place), :].astype(WIDE) + arrived(unit, place)
+                r.partial[unit, kept(place), :] = value.astype(SLIM)
+            to_left(unit, place).start()
+
+    def finish(unit, here):
+        value = r.partial[unit, kept(here), :].astype(WIDE)
+        if here > 0:
+            value = value + arrived(unit, here + 1)
+        if here < 3:
+            value = value + arrived(unit, here)
+        r.staged[unit] = value
+        store_unit(unit).start()
+
+    def advance(i, carry):
+        @pl.when(i < UNITS)
+        def _():
+            sum_y(i)
+
+            @pl.when(z == 0)
+            def _():
+                go_right(i, 0)
+
+            @pl.when(z == 3)
+            def _():
+                go_left(i, 3)
+
+        @pl.when((i >= 1) & (i < UNITS + 1))
+        def _():
+            @pl.when(z == 1)
+            def _():
+                go_right(i - 1, 1)
+
+            @pl.when(z == 2)
+            def _():
+                go_left(i - 1, 2)
+
+        @pl.when((i >= 2) & (i < UNITS + 2))
+        def _():
+            @pl.when(z == 1)
+            def _():
+                go_left(i - 2, 1)
+
+            @pl.when(z == 2)
+            def _():
+                go_right(i - 2, 2)
+
+        @pl.when(i >= 3)
+        def _():
+            for here in range(4):
+
+                @pl.when(z == here)
+                def _():
+                    finish(i - 3, here)
+
+        @pl.when(i == 5)
+        def _():
+            norm_to_y().wait_recv()
+            r.norms[4] = r.norms[2] + r.norms[3]
+            for hop in (1, 2, 3):
+                norm_to_z(hop).start()
+
+        @pl.when(i == 11)
+        def _():
+            for hop in (1, 2, 3):
+                norm_to_z(hop).wait_recv()
+            r.norms[0] = (r.norms[4] + r.norms[5]) + (r.norms[6] + r.norms[7])
+
+        return carry
+
+    norm_to_pair().wait_send()
+    lax.fori_loop(0, UNITS + 3, advance, 0)
+    store_norms = local(r.norms.at[0], r.out_norms, r.store_sem.at[2, 0])
+    store_norms.start()
+
+    norm_to_y().wait_send()
+    for hop in (1, 2, 3):
+        norm_to_z(hop).wait_send()
+    share_acts(1).wait_send()
+    for micro in range(2):
+        share_branch(micro).wait_send()
+        share_grads(micro).wait_send()
+        store_result(micro).wait()
+        store_grad(micro).wait()
+
+        @pl.when(leading)
+        def _():
+            relay_up(micro).wait_send()
+
+        @pl.when(jnp.logical_not(leading))
+        def _():
+            relay_back(micro).wait_send()
+
+    def drain(unit, carry):
+        to_y(unit).wait_send()
+        for index in range(3):
+            remote(
+                r.partial.at[unit, kept(0)], r.z_in.at[unit, 0], r.z_send.at[unit, index], r.z_recv.at[unit, 0], section, dp
+            ).wait_send()
+        store_unit(unit).wait()
+        return carry
+
+    lax.fori_loop(0, UNITS, drain, 0)
+    store_norms.wait()
+
+
+def step_on_device(
+    inputs, clip_lengths, anchor_offsets, cotangent, inward_weight, outward_weight, up_weight, down_weight, norm_gain, norm_bias
+):
+    _, _, length, width = inputs.shape
+    wide_ff = up_weight.shape[2]
+    anywhere = pl.BlockSpec(memory_space=pl.ANY)
+    in_vmem = pl.BlockSpec(memory_space=pltpu.VMEM)
+    in_smem = pl.BlockSpec(memory_space=pltpu.SMEM)
+    dma = pltpu.SemaphoreType.DMA
+    results, grads, units, norms = pl.pallas_call(
+        step_kernel,
+        out_shape=(
+            jax.ShapeDtypeStruct((2, length, width), SLIM),
+            jax.ShapeDtypeStruct((2, length, width), WIDE),
+            jax.ShapeDtypeStruct((UNITS, BLOCK, width), WIDE),
+            jax.ShapeDtypeStruct((8, width), WIDE),
+        ),
+        in_specs=[anywhere] * 6 + [in_vmem] * 2 + [in_smem] * 2,
+        out_specs=[anywhere] * 4,
+        scratch_shapes=[
+            pltpu.VMEM((2, length, width), SLIM),
+            pltpu.VMEM((width, 3 * width), SLIM),
+            pltpu.VMEM((width, width), SLIM),
+            pltpu.VMEM((width, wide_ff), SLIM),
+            pltpu.VMEM((wide_ff, width), SLIM),
+            pltpu.VMEM((9, 4 * length, width), SLIM),
+            pltpu.VMEM((7, 8 * BLOCK, 4 * length), SLIM),
+            pltpu.VMEM((7, 8 * BLOCK, length), SLIM),
+            pltpu.VMEM((2, width // HEAD, length, length), SLIM),
+            pltpu.VMEM((2, length, width), WIDE),
+            pltpu.VMEM((length, width), SLIM),
+            pltpu.VMEM((length, width), SLIM),
+            pltpu.VMEM((width, length), SLIM),
+            pltpu.VMEM((length, width), WIDE),
+            pltpu.VMEM((2, length, width), SLIM),
+            pltpu.VMEM((2, length, width), SLIM),
+            pltpu.VMEM((4, 8, width), WIDE),
+            pltpu.VMEM((length, length), WIDE),
+            pltpu.VMEM((UNITS, 8 * BLOCK, width), SLIM),
+            pltpu.VMEM((UNITS, 4 * BLOCK, width), SLIM),
+            pltpu.VMEM((UNITS, 5, BLOCK, width), SLIM),
+            pltpu.VMEM((UNITS, BLOCK, width), WIDE),
+            pltpu.VMEM((8, 8, width), WIDE),
+            dma((4,)), dma((2,)), dma((3, 2)), dma((UNITS,)),
+            dma((2,)), dma((2,)), dma((2,)), dma((2,)), dma((2,)), dma((2,)), dma((2,)), dma((2,)),
+            dma((UNITS,)), dma((UNITS,)), dma((UNITS, 3)), dma((UNITS, 5)), dma((5,)), dma((5,)),
+        ],
+        compiler_params=pltpu.CompilerParams(
+            collective_id=0, has_side_effects=True, vmem_limit_bytes=VMEM_BYTES
+        ),
+    )(
+        inputs, cotangent, inward_weight, outward_weight, up_weight, down_weight,
+        norm_gain, norm_bias, clip_lengths, anchor_offsets,
+    )
+    share = width // lax.axis_size("dp")
+    mine = lax.dynamic_slice(norms, (0, lax.axis_index("dp") * share), (4, share))
+
+    def side_by_side(some):
+        return some.transpose(1, 0, 2).reshape(1, BLOCK, -1)
+
+    return (
+        results[None, :, None],
+        grads[None, :, None],
+        side_by_side(units[9:12]),
+        units[8:9],
+        side_by_side(units[4:8]),
+        units[0:4].reshape(1, 4 * BLOCK, width),
+        mine[None, 0:2],
+        mine[None, 2:4],
+    )
 
 
 def shifted(x, axis, by):
@@ -320,8 +946,9 @@
 
 
 def solution(mesh):
+    local = step_on_device if mesh.shape["dp"] == 16 and mesh.shape["section"] == 2 else per_device
     return jax.shard_map(
-        per_device,
+        local,
         mesh=mesh,
         in_specs=(
             P(None, "dp", None, None),

time: 737 us -> 174 us (0.24); the launches traced: 727 us -> 174 us
  waiting for transfers between devices: 334 us -> 0 us
  Pallas kernels: 0 us -> 162 us
  other arithmetic: 127 us -> 0 us
  matrix products: 91 us -> 0 us
  local copies, waits for them, and re-layouts: 91.3 us -> 11 us
  blocking collectives: 59.5 us -> 0 us
  between operations: 15.6 us -> 0.67 us
    reduce_scatter x4 -> x0, waiting for transfers between devices: 279 us -> none  [the longest x1 116 us: per_device(): lax.psum_scatter(up_sum, 'dp', scatter_dimension=0, tiled=True)]
    pallas_call x0 -> x1, Pallas kernels: none -> 162 us  [step_on_device(): pl.pallas_call(step_kernel, out_shape=(jax.ShapeDtypeStruct((2, length, w...]
    dot_general x38 -> x0, matrix products: 91 us -> none  [the longest x8 22.4 us: contract_cols(): lax.dot_general(left, right, (((1,), (1,)), ((), ())), preferred_element_...]
    unnamed x1 -> x0, blocking collectives: 59.5 us -> none
    ppermute x4 -> x0, waiting for transfers between devices: 54.6 us -> none  [shifted(): return lax.ppermute(x, axis, pairs)]
    add x15 -> x0, other arithmetic: 53.7 us -> none  [the longest x1 15.2 us: per_device(): up_sum = up_sum + feed_part[0]]
    dynamic_update_slice x31 -> x0, other arithmetic: 42.5 us -> none  [update(): lax.dynamic_update_index_in_dim(element, jnp.where(working, fresh, former...]
    unnamed x163 -> x6, local copies, waits for them, and re-layouts: 26.4 us -> 2.03 us
  transfers between devices with their start and end apart: 8 -> 0, of which waited for: 5 -> 0; matrix products, arithmetic and copies ran while one was open for 14% -> 0% of each run, Pallas kernels for 0% -> 0%
where the time goes in v1:
time: 174 us
  Pallas kernels  162 us (93%)
  local copies, waits for them, and re-layouts  11 us (6%)
    pallas_call x1, Pallas kernels, step_on_device(): pl.pallas_call(step_kernel, out_shape=(jax.ShapeDtypeStruct((2, length, w...  162 us

profile of v1, /device:TPU:0, one launch (start us, length us, event | category | flops | bytes accessed | tf_op | source)
XLA Modules:
  0.0 173.5 jit_solution(11621661076060844336)
XLA Ops:
  0.6 161.9 %shard_map.161 = (bf16[2,256,768]{2,1,0:T(8,128)(2,1)}, f32[2,256,768]{2,1,0:T(8,128)}, f32[12,48,768]{2,1,0:T(8,128)}, f32[8,768]{1,0:T(8,128)}) custom-call(bf16[2,1,256,768]{3,2,1,0:T(8,128)(2,1)} %refs_0_.1, bf16[2,1,256,768]{3,2,1,0:T(8,128)(2,1)} %refs_1_.1, bf16[1,768,2304]{2,1,0:T(8,128)(2,1)} %refs_2_.1, bf16[1,768,768]{2,1,0:T(8,128)(2,1)} %refs_3_.1, ...), custom_call_target="tpu_custom_call" | custom-call | tf_op jit(solution)/shard_map/pallas_call | solution.py:575
  162.5 0.8 constant_dynamic-slice_fusion
  163.3 0.6 slice_bitcast_fusion.2
  163.9 1.6 slice.19
  165.4 1.0 slice_bitcast_fusion.1
  166.5 2.1 %fusion = (f32[4,48,768]{2,1,0:T(8,128)}, f32[48,4,768]{2,0,1:T(8,128)S(1)}) fusion(f32[12,48,768]{2,1,0:T(8,128)} %get-tuple-element.14), kind=kLoop, calls=%fused_computation.5 | loop fusion | bytes 2359296 | tf_op jit(solution)/shard_map/slice | solution.py:632
  168.6 0.3 copy.20
  168.9 0.0 copy-start.1
  168.9 1.1 reshape.25
  170.0 0.0 copy-start
  170.0 0.4 copy.21
  170.4 1.1 reshape.26
  171.5 0.0 copy-done.1
  171.5 0.9 copy.26
  172.4 0.0 copy-done
  172.4 1.1 copy.27
Async XLA Ops:
  168.9 2.6 %copy-start.1 = (bf16[2,256,768]{2,1,0:T(8,128)(2,1)S(1)}, bf16[2,256,768]{2,1,0:T(8,128)(2,1)}, u32[]{:S(2)}) copy-start(bf16[2,256,768]{2,1,0:T(8,128)(2,1)} %get-tuple-element.12) | copy-start | bytes 2359300
  170.0 2.4 %copy-start = (f32[2,256,768]{2,1,0:T(8,128)S(1)}, f32[2,256,768]{2,1,0:T(8,128)}, u32[]{:S(2)}) copy-start(f32[2,256,768]{2,1,0:T(8,128)} %get-tuple-element.13) | copy-start | bytes 4718596

commit v2 on v1

--- a/solution.py
+++ b/solution.py
@@ -15,8 +15,12 @@
 SLIM = jnp.bfloat16
 VMEM_BYTES = 67043328
 
-UNITS = 12
+UNITS = 24
+FAR = 4
+NEAR = UNITS - FAR
+EARLY = 8
 BLOCK = 48
+COLUMNS = 384
 
 
 def times(left, right):
@@ -212,13 +216,13 @@
 
 NAMES = (
     "x_in", "cot_in", "inward_in", "outward_in", "up_in", "down_in", "gain", "bias", "lengths", "offsets",
-    "out_result", "out_grad", "out_weights", "out_norms",
+    "out_result", "out_grad", "out_down", "out_up", "out_outward", "out_inward", "out_norms",
     "stream", "inward", "outward", "up", "down", "grads", "acts", "acts_out", "weights", "middle", "normed", "held",
     "turned", "total", "result", "passed", "sums", "bias_mask",
-    "partial", "y_in", "z_in", "staged", "norms",
+    "partial", "y_in", "z_in", "far_y_in", "far_z_in", "staged", "norms",
     "load_sem", "source_sem", "store_sem", "unit_sem",
     "relay_send", "relay_recv", "acts_send", "acts_recv", "branch_send", "branch_recv", "grads_send", "grads_recv",
-    "y_send", "y_recv", "z_send", "z_recv", "norm_send", "norm_recv",
+    "y_send", "y_recv", "z_send", "z_recv", "far_y_send", "far_y_recv", "far_z_send", "far_z_recv", "norm_send", "norm_recv",
 )
 
 
@@ -286,25 +290,54 @@
         return local(r.middle.at[micro], r.out_grad.at[micro], r.store_sem.at[1, micro])
 
     def to_y(unit):
-        return remote(r.partial.at[unit, 0:192], r.y_in.at[unit], r.y_send.at[unit], r.y_recv.at[unit], section, y_dp)
-
-    def kept(place):
-        return pl.ds(192 + BLOCK * place, BLOCK)
-
-    def to_right(unit, place):
         return remote(
-            r.partial.at[unit, kept(place)], r.z_in.at[unit, place + 1],
-            r.z_send.at[unit, place - 1], r.z_recv.at[unit, place + 1], section, dp + 4,
-        )
-
-    def to_left(unit, place):
+            r.partial.at[unit, 0], r.y_in.at[unit - FAR], r.y_send.at[unit - FAR], r.y_recv.at[unit - FAR], section, y_dp
+        )
+
+    def rows_of(place):
+        return pl.ds(BLOCK * place, BLOCK)
+
+    def near_z(unit, place, index, lane, to_dp):
+        near = unit - FAR
         return remote(
-            r.partial.at[unit, kept(place)], r.z_in.at[unit, place],
-            r.z_send.at[unit, place], r.z_recv.at[unit, place], section, dp - 4,
+            r.partial.at[unit, 1, rows_of(place)], r.z_in.at[near, index],
+            r.z_send.at[near, lane], r.z_recv.at[near, index], section, to_dp,
+        )
+
+    def far_z(unit, place, index, lane, to_dp):
+        return remote(
+            r.partial.at[unit, :, rows_of(place)], r.far_z_in.at[unit, index],
+            r.far_z_send.at[unit, lane], r.far_z_recv.at[unit, index], section, to_dp,
+        )
+
+    def far_to_y(unit, place):
+        return remote(
+            r.partial.at[unit, 0, rows_of(place)], r.far_y_in.at[unit], r.far_y_send.at[unit], r.far_y_recv.at[unit], section, y_dp
         )
 
     def store_unit(unit):
-        return local(r.staged.at[unit], r.out_weights.at[unit], r.unit_sem.at[unit])
+        source, sem = r.staged.at[unit], r.unit_sem.at[unit]
+
+        def part(out, base):
+            return local(source, out.at[:, pl.ds(pl.multiple_of((unit - base) * COLUMNS, 128), COLUMNS)], sem)
+
+        @pl.when(unit < 8)
+        def _():
+            rows = pl.ds(pl.multiple_of(lax.div(unit, 2) * BLOCK, 16), BLOCK)
+            cols = pl.ds(pl.multiple_of(lax.rem(unit, 2) * COLUMNS, 128), COLUMNS)
+            local(source, r.out_down.at[rows, cols], sem).start()
+
+        @pl.when((unit >= 8) & (unit < 16))
+        def _():
+            part(r.out_up, 8).start()
+
+        @pl.when((unit >= 16) & (unit < 18))
+        def _():
+            part(r.out_outward, 16).start()
+
+        @pl.when(unit >= 18)
+        def _():
+            part(r.out_inward, 18).start()
 
     r.load_inward.start()
 
@@ -328,27 +361,96 @@
     peers += [(section, lax.rem(dp + 4 * hop, 16)) for hop in (1, 2, 3)]
     for peer in peers:
         pl.semaphore_signal(barrier, inc=1, device_id=peer, device_id_type=MESH)
-    pl.semaphore_wait(barrier, len(peers))
+
+    def everyone_in():
+        pl.semaphore_wait(barrier, len(peers))
 
     def arrive(micro):
         relay_back(micro).wait_recv()
         share_branch(micro).start()
 
-    def weight_unit(unit):
-        slab = jnp.minimum(unit, 4) + jnp.where(unit >= 8, 1, 0) + jnp.where(unit >= 9, 1, 0)
-        column = jnp.maximum(unit - 3, 0)
+    def weight_operands(unit):
+        whole = lax.div(unit, 2)
+        slab = jnp.minimum(whole, 4) + jnp.where(whole >= 8, 1, 0) + jnp.where(whole >= 9, 1, 0)
+        cols = pl.ds(pl.multiple_of(lax.rem(unit, 2) * COLUMNS, 128), COLUMNS)
         other = pl.ds(pl.multiple_of((1 - y) * 192, 64), 192)
         own = pl.ds(pl.multiple_of(y * 192, 64), 192)
-        r.partial[unit, 0:192, :] = times(r.acts[slab, other, :], r.grads[column]).astype(SLIM)
+        return slab, other, own, r.grads[jnp.maximum(whole - 3, 0), :, cols]
+
+    def near_unit(unit):
+        slab, other, own, grads = weight_operands(unit)
+        r.partial[unit, 0] = times(r.acts[slab, other, :], grads).astype(SLIM)
         to_y(unit).start()
-        r.partial[unit, 192:384, :] = times(r.acts[slab, own, :], r.grads[column]).astype(SLIM)
-
-    def weight_units(low, high):
-        def body(unit, carry):
-            weight_unit(unit)
-            return carry
-
-        lax.fori_loop(low, high, body, 0)
+        r.partial[unit, 1] = times(r.acts[slab, own, :], grads).astype(SLIM)
+
+    def far_unit(unit):
+        slab, other, own, grads = weight_operands(unit)
+        r.partial[unit, 0] = times(r.acts[slab, other, :], grads).astype(SLIM)
+        r.partial[unit, 1] = times(r.acts[slab, own, :], grads).astype(SLIM)
+        at_ends(unit, far_z, r.far_z_in)
+
+    def arrived(unit, index, copy, into):
+        copy(unit, 0, index, 0, dp).wait_recv()
+        return into[unit if into is r.far_z_in else unit - FAR, index].astype(WIDE)
+
+    def pick(unit, place, copy):
+        return (unit, slice(None) if copy is far_z else 1, rows_of(place))
+
+    def go_right(unit, here, copy, into):
+        for place in range(3, here, -1):
+            at = pick(unit, place, copy)
+            if here > 0:
+                r.partial[at] = (r.partial[at].astype(WIDE) + arrived(unit, place + 1, copy, into)).astype(SLIM)
+            copy(unit, place, place + 1, place - 1, dp + 4).start()
+
+    def go_left(unit, here, copy, into):
+        for place in range(here):
+            at = pick(unit, place, copy)
+            if here < 3:
+                r.partial[at] = (r.partial[at].astype(WIDE) + arrived(unit, place, copy, into)).astype(SLIM)
+            copy(unit, place, place, place, dp - 4).start()
+
+    def at_ends(unit, copy, into):
+        @pl.when(z == 0)
+        def _():
+            go_right(unit, 0, copy, into)
+
+        @pl.when(z == 3)
+        def _():
+            go_left(unit, 3, copy, into)
+
+    def at_middle_first(unit, copy, into):
+        @pl.when(z == 1)
+        def _():
+            go_right(unit, 1, copy, into)
+
+        @pl.when(z == 2)
+        def _():
+            go_left(unit, 2, copy, into)
+
+    def at_middle_second(unit, copy, into):
+        @pl.when(z == 1)
+        def _():
+            go_left(unit, 1, copy, into)
+
+        @pl.when(z == 2)
+        def _():
+            go_right(unit, 2, copy, into)
+
+    def gathered(unit, here, copy, into):
+        value = r.partial[pick(unit, here, copy)].astype(WIDE)
+        if here > 0:
+            value = value + arrived(unit, here + 1, copy, into)
+        if here < 3:
+            value = value + arrived(unit, here, copy, into)
+        return value
+
+    def everywhere(action):
+        for here in range(4):
+
+            @pl.when(z == here)
+            def _():
+                action(here)
 
     def slot(t, carry):
         trailing = jnp.logical_not(leading)
@@ -359,6 +461,7 @@
 
         @pl.when(trailing & (t == 0))
         def _():
+            everyone_in()
             for micro in range(2):
                 load_cot(micro).wait()
                 share_branch(micro).start()
@@ -377,6 +480,10 @@
 
             forward(r, micro, pl.multiple_of((c * 2 + micro) * length, length), t == section)
 
+            @pl.when(leading & (t == 0))
+            def _():
+                everyone_in()
+
             @pl.when(leading)
             def _():
                 relay_up(micro).start()
@@ -409,7 +516,13 @@
             for micro in range(2):
                 share_branch(micro, 1 - c).wait_recv()
                 share_acts(micro, 1 - c).wait_recv()
-            weight_units(0, 4)
+
+            def body(i, carry):
+                near_unit(FAR + i)
+                far_unit(i)
+                return carry
+
+            lax.fori_loop(0, FAR, body, 0)
 
         return carry
 
@@ -434,103 +547,84 @@
     norm_to_y().start()
     for micro in range(2):
         share_grads(micro, 1 - c).wait_recv()
-    weight_units(4, UNITS)
 
     def sum_y(unit):
         to_y(unit).wait_recv()
-        r.partial[unit, 192:384, :] = (
-            r.partial[unit, 192:384, :].astype(WIDE) + r.y_in[unit].astype(WIDE)
-        ).astype(SLIM)
-
-    def arrived(unit, index):
-        remote(
-            r.partial.at[unit, kept(0)], r.z_in.at[unit, index], r.z_send.at[unit, 0], r.z_recv.at[unit, index], section, dp
-        ).wait_recv()
-        return r.z_in[unit, index].astype(WIDE)
-
-    def go_right(unit, here):
-        for place in range(3, here, -1):
-            if here > 0:
-                value = r.partial[unit, kept(place), :].astype(WIDE) + arrived(unit, place + 1)
-                r.partial[unit, kept(place), :] = value.astype(SLIM)
-            to_right(unit, place).start()
-
-    def go_left(unit, here):
-        for place in range(here):
-            if here < 3:
-                value = r.partial[unit, kept(place), :].astype(WIDE) + arrived(unit, place)
-                r.partial[unit, kept(place), :] = value.astype(SLIM)
-            to_left(unit, place).start()
-
-    def finish(unit, here):
-        value = r.partial[unit, kept(here), :].astype(WIDE)
-        if here > 0:
-            value = value + arrived(unit, here + 1)
-        if here < 3:
-            value = value + arrived(unit, here)
-        r.staged[unit] = value
-        store_unit(unit).start()
+        r.partial[unit, 1] = (r.partial[unit, 1].astype(WIDE) + r.y_in[unit - FAR].astype(WIDE)).astype(SLIM)
 
     def advance(i, carry):
-        @pl.when(i < UNITS)
-        def _():
-            sum_y(i)
-
-            @pl.when(z == 0)
-            def _():
-                go_right(i, 0)
-
-            @pl.when(z == 3)
-            def _():
-                go_left(i, 3)
-
-        @pl.when((i >= 1) & (i < UNITS + 1))
-        def _():
-            @pl.when(z == 1)
-            def _():
-                go_right(i - 1, 1)
-
-            @pl.when(z == 2)
-            def _():
-                go_left(i - 1, 2)
-
-        @pl.when((i >= 2) & (i < UNITS + 2))
-        def _():
-            @pl.when(z == 1)
-            def _():
-                go_left(i - 2, 1)
-
-            @pl.when(z == 2)
-            def _():
-                go_right(i - 2, 2)
+        @pl.when(i < UNITS - EARLY)
+        def _():
+            near_unit(EARLY + i)
+
+        @pl.when(i < NEAR)
+        def _():
+            sum_y(FAR + i)
+            at_ends(FAR + i, near_z, r.z_in)
+
+        half = lax.div(i, 2)
+        odd = lax.rem(i, 2) == 1
+
+        @pl.when(odd & (i < 2 * FAR))
+        def _():
+            at_middle_first(half, far_z, r.far_z_in)
+
+        @pl.when(jnp.logical_not(odd) & (i >= 4) & (i < 4 + 2 * FAR))
+        def _():
+            at_middle_second(half - 2, far_z, r.far_z_in)
+
+        @pl.when(odd & (i >= 7) & (i < 7 + 2 * FAR))
+        def _():
+            def action(here):
+                unit = half - 3
+                value = gathered(unit, here, far_z, r.far_z_in)
+                r.partial[unit, 0, rows_of(here)] = value[0].astype(SLIM)
+                far_to_y(unit, here).start()
+                r.staged[unit] = value[1]
+
+            everywhere(action)
+
+        @pl.when(jnp.logical_not(odd) & (i >= 10) & (i < 10 + 2 * FAR))
+        def _():
+            unit = half - 5
+            far_to_y(unit, 0).wait_recv()
+            r.staged[unit] += r.far_y_in[unit].astype(WIDE)
+            store_unit(unit)
+
+        @pl.when((i >= 1) & (i < NEAR + 1))
+        def _():
+            at_middle_first(FAR + i - 1, near_z, r.z_in)
+
+        @pl.when((i >= 2) & (i < NEAR + 2))
+        def _():
+            at_middle_second(FAR + i - 2, near_z, r.z_in)
 
         @pl.when(i >= 3)
         def _():
-            for here in range(4):
-
-                @pl.when(z == here)
-                def _():
-                    finish(i - 3, here)
-
-        @pl.when(i == 5)
+            def action(here):
+                r.staged[FAR + i - 3] = gathered(FAR + i - 3, here, near_z, r.z_in)
+
+            everywhere(action)
+            store_unit(FAR + i - 3)
+
+        @pl.when(i == 4)
         def _():
             norm_to_y().wait_recv()
             r.norms[4] = r.norms[2] + r.norms[3]
             for hop in (1, 2, 3):
                 norm_to_z(hop).start()
 
-        @pl.when(i == 11)
+        @pl.when(i == 18)
         def _():
             for hop in (1, 2, 3):
                 norm_to_z(hop).wait_recv()
             r.norms[0] = (r.norms[4] + r.norms[5]) + (r.norms[6] + r.norms[7])
+            local(r.norms.at[0], r.out_norms, r.store_sem.at[2, 0]).start()
 
         return carry
 
     norm_to_pair().wait_send()
-    lax.fori_loop(0, UNITS + 3, advance, 0)
-    store_norms = local(r.norms.at[0], r.out_norms, r.store_sem.at[2, 0])
-    store_norms.start()
+    lax.fori_loop(0, NEAR + 3, advance, 0)
 
     norm_to_y().wait_send()
     for hop in (1, 2, 3):
@@ -550,17 +644,50 @@
         def _():
             relay_back(micro).wait_send()
 
-    def drain(unit, carry):
-        to_y(unit).wait_send()
-        for index in range(3):
-            remote(
-                r.partial.at[unit, kept(0)], r.z_in.at[unit, 0], r.z_send.at[unit, index], r.z_recv.at[unit, 0], section, dp
-            ).wait_send()
-        store_unit(unit).wait()
+    def drain_near(near, carry):
+        to_y(FAR + near).wait_send()
+        for lane in range(3):
+            near_z(FAR + near, 0, 0, lane, dp).wait_send()
         return carry
 
-    lax.fori_loop(0, UNITS, drain, 0)
-    store_norms.wait()
+    lax.fori_loop(0, NEAR, drain_near, 0)
+
+    def drain_far(unit, carry):
+        far_to_y(unit, 0).wait_send()
+        for lane in range(3):
+            far_z(unit, 0, 0, lane, dp).wait_send()
+        return carry
+
+    lax.fori_loop(0, FAR, drain_far, 0)
+
+    def drain_store(unit, carry):
+        local(r.staged.at[unit], r.out_outward.at[:, 0:COLUMNS], r.unit_sem.at[unit]).wait()
+        return carry
+
+    lax.fori_loop(0, UNITS, drain_store, 0)
+    local(r.norms.at[0], r.out_norms, r.store_sem.at[2, 0]).wait()
+
+
+def hand_over_kernel(*refs):
+    sources, norms, targets = refs[:6], refs[6], refs[7:13]
+    gain_grad, bias_grad, held, in_sem, out_sem = refs[13], refs[14], refs[15:21], refs[21], refs[22]
+    loads = [pltpu.make_async_copy(a, b, in_sem.at[k]) for k, (a, b) in enumerate(zip(sources, held))]
+    stores = [pltpu.make_async_copy(a, b, out_sem.at[k]) for k, (a, b) in enumerate(zip(held, targets))]
+    for load in loads:
+        load.start()
+    share = gain_grad.shape[2]
+    for index in range(norms.shape[1] // share):
+
+        @pl.when(lax.axis_index("dp") == index)
+        def _():
+            gain_grad[0] = norms[0:2, index * share : (index + 1) * share]
+            bias_grad[0] = norms[2:4, index * share : (index + 1) * share]
+
+    for load, store in zip(loads, stores):
+        load.wait()
+        store.start()
+    for store in stores:
+        store.wait()
 
 
 def step_on_device(
@@ -572,16 +699,20 @@
     in_vmem = pl.BlockSpec(memory_space=pltpu.VMEM)
     in_smem = pl.BlockSpec(memory_space=pltpu.SMEM)
     dma = pltpu.SemaphoreType.DMA
-    results, grads, units, norms = pl.pallas_call(
+    share = width // lax.axis_size("dp")
+    shapes = [
+        jax.ShapeDtypeStruct((2, length, width), SLIM),
+        jax.ShapeDtypeStruct((2, length, width), WIDE),
+        jax.ShapeDtypeStruct((4 * BLOCK, width), WIDE),
+        jax.ShapeDtypeStruct((BLOCK, wide_ff), WIDE),
+        jax.ShapeDtypeStruct((BLOCK, width), WIDE),
+        jax.ShapeDtypeStruct((BLOCK, 3 * width), WIDE),
+    ]
+    made = pl.pallas_call(
         step_kernel,
-        out_shape=(
-            jax.ShapeDtypeStruct((2, length, width), SLIM),
-            jax.ShapeDtypeStruct((2, length, width), WIDE),
-            jax.ShapeDtypeStruct((UNITS, BLOCK, width), WIDE),
-            jax.ShapeDtypeStruct((8, width), WIDE),
-        ),
+        out_shape=(*shapes, jax.ShapeDtypeStruct((8, width), WIDE)),
         in_specs=[anywhere] * 6 + [in_vmem] * 2 + [in_smem] * 2,
-        out_specs=[anywhere] * 4,
+        out_specs=[anywhere] * 7,
         scratch_shapes=[
             pltpu.VMEM((2, length, width), SLIM),
             pltpu.VMEM((width, 3 * width), SLIM),
@@ -601,14 +732,17 @@
             pltpu.VMEM((2, length, width), SLIM),
             pltpu.VMEM((4, 8, width), WIDE),
             pltpu.VMEM((length, length), WIDE),
-            pltpu.VMEM((UNITS, 8 * BLOCK, width), SLIM),
-            pltpu.VMEM((UNITS, 4 * BLOCK, width), SLIM),
-            pltpu.VMEM((UNITS, 5, BLOCK, width), SLIM),
-            pltpu.VMEM((UNITS, BLOCK, width), WIDE),
+            pltpu.VMEM((UNITS, 2, 4 * BLOCK, COLUMNS), SLIM),
+            pltpu.VMEM((NEAR, 4 * BLOCK, COLUMNS), SLIM),
+            pltpu.VMEM((NEAR, 5, BLOCK, COLUMNS), SLIM),
+            pltpu.VMEM((FAR, BLOCK, COLUMNS), SLIM),
+            pltpu.VMEM((FAR, 5, 2, BLOCK, COLUMNS), SLIM),
+            pltpu.VMEM((UNITS, BLOCK, COLUMNS), WIDE),
             pltpu.VMEM((8, 8, width), WIDE),
             dma((4,)), dma((2,)), dma((3, 2)), dma((UNITS,)),
             dma((2,)), dma((2,)), dma((2,)), dma((2,)), dma((2,)), dma((2,)), dma((2,)), dma((2,)),
-            dma((UNITS,)), dma((UNITS,)), dma((UNITS, 3)), dma((UNITS, 5)), dma((5,)), dma((5,)),
+            dma((NEAR,)), dma((NEAR,)), dma((NEAR, 3)), dma((NEAR, 5)),
+            dma((FAR,)), dma((FAR,)), dma((FAR, 3)), dma((FAR, 5)), dma((5,)), dma((5,)),
         ],
         compiler_params=pltpu.CompilerParams(
             collective_id=0, has_side_effects=True, vmem_limit_bytes=VMEM_BYTES
@@ -617,21 +751,22 @@
         inputs, cotangent, inward_weight, outward_weight, up_weight, down_weight,
         norm_gain, norm_bias, clip_lengths, anchor_offsets,
     )
-    share = width // lax.axis_size("dp")
-    mine = lax.dynamic_slice(norms, (0, lax.axis_index("dp") * share), (4, share))
-
-    def side_by_side(some):
-        return some.transpose(1, 0, 2).reshape(1, BLOCK, -1)
-
+    result, grad, down, up, outward, inward, gain_grad, bias_grad = pl.pallas_call(
+        hand_over_kernel,
+        out_shape=(*shapes, *[jax.ShapeDtypeStruct((1, 2, share), WIDE)] * 2),
+        in_specs=[anywhere] * 6 + [in_vmem],
+        out_specs=[anywhere] * 6 + [in_vmem] * 2,
+        scratch_shapes=[pltpu.VMEM(shape.shape, shape.dtype) for shape in shapes] + [dma((6,)), dma((6,))],
+    )(*made)
     return (
-        results[None, :, None],
-        grads[None, :, None],
-        side_by_side(units[9:12]),
-        units[8:9],
-        side_by_side(units[4:8]),
-        units[0:4].reshape(1, 4 * BLOCK, width),
-        mine[None, 0:2],
-        mine[None, 2:4],
+        result[None, :, None],
+        grad[None, :, None],
+        inward[None],
+        outward[None],
+        up[None],
+        down[None],
+        gain_grad,
+        bias_grad,
     )
 
 

time: 174 us -> 162 us (0.931)
  local copies, waits for them, and re-layouts: 11 us -> 0 us
    slice x2 -> x0, local copies, waits for them, and re-layouts: 3.72 us -> none  [the longest x1 2.14 us: step_on_device(): units[0:4].reshape(1, 4 * BLOCK, width)]
    reshape x2 -> x0, local copies, waits for them, and re-layouts: 2.19 us -> none  [side_by_side(): return some.transpose(1, 0, 2).reshape(1, BLOCK, -1)]
    unnamed x6 -> x0, local copies, waits for them, and re-layouts: 2.03 us -> none
    pallas_call x1 -> x2, Pallas kernels: 162 us -> 161 us  [the longest x1 157 us: step_on_device(): pl.pallas_call(step_kernel, out_shape=(*shapes, jax.ShapeDtypeStruct((8,...]
where the time goes in v2:
time: 162 us
  Pallas kernels  161 us (99%)
    pallas_call x1, Pallas kernels, step_on_device(): pl.pallas_call(step_kernel, out_shape=(*shapes, jax.ShapeDtypeStruct((8,...  157 us
    pallas_call x1, Pallas kernels, step_on_device(): pl.pallas_call(hand_over_kernel, out_shape=(*shapes, *[jax.ShapeDtypeStru...  4.78 us

profile of v2, /device:TPU:0, one launch (start us, length us, event | category | flops | bytes accessed | tf_op | source)
XLA Modules:
  0.0 162.0 jit_solution(7326679480059131070)
XLA Ops:
  0.6 156.6 %shard_map.161 = (bf16[2,256,768]{2,1,0:T(8,128)(2,1)}, f32[2,256,768]{2,1,0:T(8,128)}, f32[192,768]{1,0:T(8,128)}, f32[48,3072]{1,0:T(8,128)}, f32[48,768]{1,0:...) custom-call(bf16[2,1,256,768]{3,2,1,0:T(8,128)(2,1)} %refs_0_.1, bf16[2,1,256,768]{3,2,1,0:T(8,128)(2,1)} %refs_1_.1, ...), custom_call_target="tpu_custom_call" | custom-call | tf_op jit(solution)/shard_map/pallas_call | solution.py:711
  157.2 4.8 %shard_map.162 = (bf16[2,256,768]{2,1,0:T(8,128)(2,1)}, f32[2,256,768]{2,1,0:T(8,128)}, f32[192,768]{1,0:T(8,128)}, f32[48,3072]{1,0:T(8,128)}, f32[48,768]{1,0:...) custom-call(bf16[2,256,768]{2,1,0:T(8,128)(2,1)} %get-tuple-element.23.refs_0_, ...), custom_call_target="tpu_custom_call" | custom-call | tf_op jit(solution)/shard_map/pallas_call | solution.py:754

commit v3 on v2

--- a/solution.py
+++ b/solution.py
@@ -18,9 +18,16 @@
 UNITS = 24
 FAR = 4
 NEAR = UNITS - FAR
-EARLY = 8
 BLOCK = 48
 COLUMNS = 384
+EARLY_NEAR = 4
+HOLD = 1
+LAGS = (2, 3, 4)
+FAR_AT = (-1, -1, 3, 8)
+FAR_FIRST = (2, 4, 10, 15)
+FAR_SECOND = (5, 15, 14, 20)
+FAR_ARRIVED = (17, 18, 20, 21)
+FAR_DONE = (20, 21, 22, 23)
 
 
 def times(left, right):
@@ -92,7 +99,7 @@
         r.acts_out[slab, rows, :] = r.turned[other, :]
 
 
-def forward(r, micro, tok, first):
+def forward(r, micro, tok, first, leading):
     length, width = r.normed.shape
     tokens = pl.ds(tok, length)
     mask_bias(r, micro)
@@ -101,6 +108,10 @@
     @pl.when(first)
     def _():
         r.load_inward.wait()
+
+        @pl.when(leading)
+        def _():
+            r.load_rest()
 
     for part in range(3):
         r.grads[6 + part, tokens, :] = times(
@@ -135,14 +146,18 @@
     @pl.when(first)
     def _():
         r.load_outward.wait()
-        r.load_up.wait()
-        r.load_down.wait()
 
     r.middle[micro] = r.stream[micro].astype(WIDE) + times(r.held[...], r.outward[...])
     r.normed[...] = norm_rows_bf16(r, r.middle[micro], 1)
     r.turned[...] = r.normed[...].T
     place(r, 4, tokens)
     r.total[...] = r.middle[micro]
+
+    @pl.when(first)
+    def _():
+        r.load_up.wait()
+        r.load_down.wait()
+
     for part in range(4):
         cols = slice(part * width, (part + 1) * width)
         lifted = times(r.normed[...], r.up[:, cols])
@@ -173,6 +188,7 @@
         lifted_grad = (hidden * r.grads[1 + part, tokens, :].astype(WIDE)).astype(SLIM)
         r.grads[1 + part, tokens, :] = lifted_grad
         r.total[...] += times_turned(lifted_grad, r.up[:, cols])
+    r.share_lifted(micro).start()
     middle_grad = r.grads[0, tokens, :].astype(WIDE) + norm_backward(
         r, r.middle[micro], r.total[...], 1
     )
@@ -221,7 +237,8 @@
     "turned", "total", "result", "passed", "sums", "bias_mask",
     "partial", "y_in", "z_in", "far_y_in", "far_z_in", "staged", "norms",
     "load_sem", "source_sem", "store_sem", "unit_sem",
-    "relay_send", "relay_recv", "acts_send", "acts_recv", "branch_send", "branch_recv", "grads_send", "grads_recv",
+    "relay_send", "relay_recv", "acts_send", "acts_recv", "branch_send", "branch_recv", "lifted_send", "lifted_recv",
+    "rest_send", "rest_recv", "turn",
     "y_send", "y_recv", "z_send", "z_recv", "far_y_send", "far_y_recv", "far_z_send", "far_z_recv", "norm_send", "norm_recv",
 )
 
@@ -252,6 +269,13 @@
     r.load_up = local(r.up_in.at[0], r.up, r.load_sem.at[2])
     r.load_down = local(r.down_in.at[0], r.down, r.load_sem.at[3])
 
+    def load_rest():
+        r.load_outward.start()
+        r.load_up.start()
+        r.load_down.start()
+
+    r.load_rest = load_rest
+
     def load_x(micro):
         return local(r.x_in.at[micro, 0], r.stream.at[micro], r.source_sem.at[micro])
 
@@ -275,12 +299,19 @@
         rows = slot_of(core, micro)
         return remote(r.grads.at[0, rows], r.grads.at[0, rows], r.branch_send.at[micro], r.branch_recv.at[micro], section, pair_dp)
 
-    def share_grads(micro, core=c):
+    def share_lifted(micro, core=c):
         rows = slot_of(core, micro)
         return remote(
-            r.grads.at[1:9, rows], r.grads.at[1:9, rows], r.grads_send.at[micro], r.grads_recv.at[micro], section, pair_dp
-        )
-
+            r.grads.at[1:5, rows], r.grads.at[1:5, rows], r.lifted_send.at[micro], r.lifted_recv.at[micro], section, pair_dp
+        )
+
+    def share_rest(micro, core=c):
+        rows = slot_of(core, micro)
+        return remote(
+            r.grads.at[5:9, rows], r.grads.at[5:9, rows], r.rest_send.at[micro], r.rest_recv.at[micro], section, pair_dp
+        )
+
+    r.share_lifted = share_lifted
     r.share_acts = share_acts
 
     def store_result(micro):
@@ -351,9 +382,10 @@
         load_cot(0).start()
         load_cot(1).start()
 
-    r.load_outward.start()
-    r.load_up.start()
-    r.load_down.start()
+    @pl.when(jnp.logical_not(leading))
+    def _():
+        r.load_rest()
+
     r.sums[...] = jnp.zeros_like(r.sums)
 
     barrier = pltpu.get_barrier_semaphore()
@@ -478,18 +510,28 @@
             def _():
                 relay_up(micro).wait_recv()
 
-            forward(r, micro, pl.multiple_of((c * 2 + micro) * length, length), t == section)
+            forward(r, micro, pl.multiple_of((c * 2 + micro) * length, length), t == section, leading)
 
             @pl.when(leading & (t == 0))
             def _():
                 everyone_in()
 
+            share_acts(micro).start()
+            store_result(micro).start()
+            ahead = leading & (c == 0) & (t == 0)
+
+            @pl.when(leading & (c == 1) & (t == 0))
+            def _():
+                pl.semaphore_wait(r.turn, 1)
+
             @pl.when(leading)
             def _():
                 relay_up(micro).start()
 
-            share_acts(micro).start()
-            store_result(micro).start()
+            @pl.when(ahead)
+            def _():
+                relay_up(0).wait_send()
+                pl.semaphore_signal(r.turn, inc=1, device_id=(section, pair_dp), device_id_type=MESH)
 
         @pl.when(leading & (t == 3))
         def _():
@@ -504,7 +546,7 @@
             def _():
                 relay_back(micro).start()
 
-            share_grads(micro).start()
+            share_rest(micro).start()
             store_grad(micro).start()
 
         @pl.when(leading & (t == 4))
@@ -517,12 +559,20 @@
                 share_branch(micro, 1 - c).wait_recv()
                 share_acts(micro, 1 - c).wait_recv()
 
+            early_far = sum(at < 0 for at in FAR_AT)
+
             def body(i, carry):
-                near_unit(FAR + i)
-                far_unit(i)
+                @pl.when(i < EARLY_NEAR)
+                def _():
+                    near_unit(FAR + i)
+
+                @pl.when(i < early_far)
+                def _():
+                    far_unit(i)
+
                 return carry
 
-            lax.fori_loop(0, FAR, body, 0)
+            lax.fori_loop(0, max(EARLY_NEAR, early_far), body, 0)
 
         return carry
 
@@ -542,41 +592,70 @@
 
     r.norms[0] = jnp.concatenate([jnp.sum(r.sums[...], 1), jnp.zeros((4, r.sums.shape[2]), WIDE)], 0)
     norm_to_pair().start()
-    norm_to_pair().wait_recv()
-    r.norms[2] = r.norms[0] + r.norms[1]
-    norm_to_y().start()
     for micro in range(2):
-        share_grads(micro, 1 - c).wait_recv()
+        share_lifted(micro, 1 - c).wait_recv()
 
     def sum_y(unit):
         to_y(unit).wait_recv()
         r.partial[unit, 1] = (r.partial[unit, 1].astype(WIDE) + r.y_in[unit - FAR].astype(WIDE)).astype(SLIM)
 
+    def far_turn(i, steps):
+        turn, unit = i < 0, jnp.int32(0)
+        for index, step in enumerate(steps):
+            if step >= 0:
+                turn = turn | (i == step)
+                unit = jnp.where(i == step, index, unit)
+        return turn, unit
+
+    def near_turn(i, lag):
+        return (i >= lag) & (i < NEAR + lag), jnp.clip(i - lag, 0, NEAR - 1) + FAR
+
     def advance(i, carry):
-        @pl.when(i < UNITS - EARLY)
-        def _():
-            near_unit(EARLY + i)
+        issued = FAR + EARLY_NEAR + i - HOLD
+
+        @pl.when(issued == 16)
+        def _():
+            for micro in range(2):
+                share_rest(micro, 1 - c).wait_recv()
+
+        @pl.when((issued >= FAR + EARLY_NEAR) & (issued < UNITS))
+        def _():
+            near_unit(issued)
+
+        turn, unit = far_turn(i, FAR_AT)
+
+        @pl.when(turn)
+        def _(unit=unit):
+            far_unit(unit)
 
         @pl.when(i < NEAR)
         def _():
             sum_y(FAR + i)
             at_ends(FAR + i, near_z, r.z_in)
 
-        half = lax.div(i, 2)
-        odd = lax.rem(i, 2) == 1
-
-        @pl.when(odd & (i < 2 * FAR))
-        def _():
-            at_middle_first(half, far_z, r.far_z_in)
-
-        @pl.when(jnp.logical_not(odd) & (i >= 4) & (i < 4 + 2 * FAR))
-        def _():
-            at_middle_second(half - 2, far_z, r.far_z_in)
-
-        @pl.when(odd & (i >= 7) & (i < 7 + 2 * FAR))
-        def _():
+        turn, unit = near_turn(i, LAGS[0])
+
+        @pl.when(turn)
+        def _(unit=unit):
+            at_middle_first(unit, near_z, r.z_in)
+
+        turn, unit = far_turn(i, FAR_FIRST)
+
+        @pl.when(turn)
+        def _(unit=unit):
+            at_middle_first(unit, far_z, r.far_z_in)
+
+        turn, unit = far_turn(i, FAR_SECOND)
+
+        @pl.when(turn)
+        def _(unit=unit):
+            at_middle_second(unit, far_z, r.far_z_in)
+
+        turn, unit = far_turn(i, FAR_ARRIVED)
+
+        @pl.when(turn)
+        def _(unit=unit):
             def action(here):
-                unit = half - 3
                 value = gathered(unit, here, far_z, r.far_z_in)
                 r.partial[unit, 0, rows_of(here)] = value[0].astype(SLIM)
                 far_to_y(unit, here).start()
@@ -584,30 +663,37 @@
 
             everywhere(action)
 
-        @pl.when(jnp.logical_not(odd) & (i >= 10) & (i < 10 + 2 * FAR))
-        def _():
-            unit = half - 5
+        turn, unit = far_turn(i, FAR_DONE)
+
+        @pl.when(turn)
+        def _(unit=unit):
             far_to_y(unit, 0).wait_recv()
             r.staged[unit] += r.far_y_in[unit].astype(WIDE)
             store_unit(unit)
 
-        @pl.when((i >= 1) & (i < NEAR + 1))
-        def _():
-            at_middle_first(FAR + i - 1, near_z, r.z_in)
-
-        @pl.when((i >= 2) & (i < NEAR + 2))
-        def _():
-            at_middle_second(FAR + i - 2, near_z, r.z_in)
-
-        @pl.when(i >= 3)
-        def _():
+        turn, unit = near_turn(i, LAGS[1])
+
+        @pl.when(turn)
+        def _(unit=unit):
+            at_middle_second(unit, near_z, r.z_in)
+
+        turn, unit = near_turn(i, LAGS[2])
+
+        @pl.when(turn)
+        def _(unit=unit):
             def action(here):
-                r.staged[FAR + i - 3] = gathered(FAR + i - 3, here, near_z, r.z_in)
+                r.staged[unit] = gathered(unit, here, near_z, r.z_in)
 
             everywhere(action)
-            store_unit(FAR + i - 3)
-
-        @pl.when(i == 4)
+            store_unit(unit)
+
+        @pl.when(i == 1)
+        def _():
+            norm_to_pair().wait()
+            r.norms[2] = r.norms[0] + r.norms[1]
+            norm_to_y().start()
+
+        @pl.when(i == 9)
         def _():
             norm_to_y().wait_recv()
             r.norms[4] = r.norms[2] + r.norms[3]
@@ -623,8 +709,7 @@
 
         return carry
 
-    norm_to_pair().wait_send()
-    lax.fori_loop(0, NEAR + 3, advance, 0)
+    lax.fori_loop(0, max(NEAR + LAGS[2], FAR_DONE[-1] + 1), advance, 0)
 
     norm_to_y().wait_send()
     for hop in (1, 2, 3):
@@ -632,11 +717,12 @@
     share_acts(1).wait_send()
     for micro in range(2):
         share_branch(micro).wait_send()
-        share_grads(micro).wait_send()
+        share_lifted(micro).wait_send()
+        share_rest(micro).wait_send()
         store_result(micro).wait()
         store_grad(micro).wait()
 
-        @pl.when(leading)
+        @pl.when(leading if micro else leading & (c == 1))
         def _():
             relay_up(micro).wait_send()
 
@@ -740,7 +826,7 @@
             pltpu.VMEM((UNITS, BLOCK, COLUMNS), WIDE),
             pltpu.VMEM((8, 8, width), WIDE),
             dma((4,)), dma((2,)), dma((3, 2)), dma((UNITS,)),
-            dma((2,)), dma((2,)), dma((2,)), dma((2,)), dma((2,)), dma((2,)), dma((2,)), dma((2,)),
+            *[dma((2,))] * 10, pltpu.SemaphoreType.REGULAR,
             dma((NEAR,)), dma((NEAR,)), dma((NEAR, 3)), dma((NEAR, 5)),
             dma((FAR,)), dma((FAR,)), dma((FAR, 3)), dma((FAR, 5)), dma((5,)), dma((5,)),
         ],

time: 162 us -> 154 us (0.951)
  Pallas kernels: 161 us -> 153 us
    pallas_call x1, Pallas kernels: 157 us -> 148 us  [step_on_device(): pl.pallas_call(step_kernel, out_shape=(*shapes, jax.ShapeDtypeStruct((8,...]
where the time goes in v3:
time: 154 us
  Pallas kernels  153 us (99%)
    pallas_call x1, Pallas kernels, step_on_device(): pl.pallas_call(step_kernel, out_shape=(*shapes, jax.ShapeDtypeStruct((8,...  148 us
    pallas_call x1, Pallas kernels, step_on_device(): pl.pallas_call(hand_over_kernel, out_shape=(*shapes, *[jax.ShapeDtypeStru...  4.78 us

profile of v3, /device:TPU:0, one launch (start us, length us, event | category | flops | bytes accessed | tf_op | source)
XLA Modules:
  0.0 153.9 jit_solution(17528623769332086599)
XLA Ops:
  0.6 148.3 %shard_map.161 = (bf16[2,256,768]{2,1,0:T(8,128)(2,1)}, f32[2,256,768]{2,1,0:T(8,128)}, f32[192,768]{1,0:T(8,128)}, f32[48,3072]{1,0:T(8,128)}, f32[48,768]{1,0:...) custom-call(bf16[2,1,256,768]{3,2,1,0:T(8,128)(2,1)} %refs_0_.1, bf16[2,1,256,768]{3,2,1,0:T(8,128)(2,1)} %refs_1_.1, ...), custom_call_target="tpu_custom_call" | custom-call | tf_op jit(solution)/shard_map/pallas_call | solution.py:797
  148.9 4.8 %shard_map.162 = (bf16[2,256,768]{2,1,0:T(8,128)(2,1)}, f32[2,256,768]{2,1,0:T(8,128)}, f32[192,768]{1,0:T(8,128)}, f32[48,3072]{1,0:T(8,128)}, f32[48,768]{1,0:...) custom-call(bf16[2,256,768]{2,1,0:T(8,128)(2,1)} %get-tuple-element.23.refs_0_, ...), custom_call_target="tpu_custom_call" | custom-call | tf_op jit(solution)/shard_map/pallas_call | solution.py:840

commit v4 on v3

--- a/solution.py
+++ b/solution.py
@@ -232,11 +232,11 @@
 
 NAMES = (
     "x_in", "cot_in", "inward_in", "outward_in", "up_in", "down_in", "gain", "bias", "lengths", "offsets",
-    "out_result", "out_grad", "out_down", "out_up", "out_outward", "out_inward", "out_norms",
-    "stream", "inward", "outward", "up", "down", "grads", "acts", "acts_out", "weights", "middle", "normed", "held",
-    "turned", "total", "result", "passed", "sums", "bias_mask",
-    "partial", "y_in", "z_in", "far_y_in", "far_z_in", "staged", "norms",
-    "load_sem", "source_sem", "store_sem", "unit_sem",
+    "result", "middle", "staged", "out_norms",
+    "stream", "inward", "outward", "up", "down", "grads", "acts", "acts_out", "weights", "normed", "held",
+    "turned", "total", "passed", "sums", "bias_mask",
+    "partial", "y_in", "z_in", "far_y_in", "far_z_in", "norms",
+    "load_sem", "source_sem",
     "relay_send", "relay_recv", "acts_send", "acts_recv", "branch_send", "branch_recv", "lifted_send", "lifted_recv",
     "rest_send", "rest_recv", "turn",
     "y_send", "y_recv", "z_send", "z_recv", "far_y_send", "far_y_recv", "far_z_send", "far_z_recv", "norm_send", "norm_recv",
@@ -314,12 +314,6 @@
     r.share_lifted = share_lifted
     r.share_acts = share_acts
 
-    def store_result(micro):
-        return local(r.result.at[micro], r.out_result.at[micro], r.store_sem.at[0, micro])
-
-    def store_grad(micro):
-        return local(r.middle.at[micro], r.out_grad.at[micro], r.store_sem.at[1, micro])
-
     def to_y(unit):
         return remote(
             r.partial.at[unit, 0], r.y_in.at[unit - FAR], r.y_send.at[unit - FAR], r.y_recv.at[unit - FAR], section, y_dp
@@ -345,30 +339,6 @@
         return remote(
             r.partial.at[unit, 0, rows_of(place)], r.far_y_in.at[unit], r.far_y_send.at[unit], r.far_y_recv.at[unit], section, y_dp
         )
-
-    def store_unit(unit):
-        source, sem = r.staged.at[unit], r.unit_sem.at[unit]
-
-        def part(out, base):
-            return local(source, out.at[:, pl.ds(pl.multiple_of((unit - base) * COLUMNS, 128), COLUMNS)], sem)
-
-        @pl.when(unit < 8)
-        def _():
-            rows = pl.ds(pl.multiple_of(lax.div(unit, 2) * BLOCK, 16), BLOCK)
-            cols = pl.ds(pl.multiple_of(lax.rem(unit, 2) * COLUMNS, 128), COLUMNS)
-            local(source, r.out_down.at[rows, cols], sem).start()
-
-        @pl.when((unit >= 8) & (unit < 16))
-        def _():
-            part(r.out_up, 8).start()
-
-        @pl.when((unit >= 16) & (unit < 18))
-        def _():
-            part(r.out_outward, 16).start()
-
-        @pl.when(unit >= 18)
-        def _():
-            part(r.out_inward, 18).start()
 
     r.load_inward.start()
 
@@ -517,7 +487,6 @@
                 everyone_in()
 
             share_acts(micro).start()
-            store_result(micro).start()
             ahead = leading & (c == 0) & (t == 0)
 
             @pl.when(leading & (c == 1) & (t == 0))
@@ -547,7 +516,6 @@
                 relay_back(micro).start()
 
             share_rest(micro).start()
-            store_grad(micro).start()
 
         @pl.when(leading & (t == 4))
         def _():
@@ -669,7 +637,6 @@
         def _(unit=unit):
             far_to_y(unit, 0).wait_recv()
             r.staged[unit] += r.far_y_in[unit].astype(WIDE)
-            store_unit(unit)
 
         turn, unit = near_turn(i, LAGS[1])
 
@@ -685,7 +652,6 @@
                 r.staged[unit] = gathered(unit, here, near_z, r.z_in)
 
             everywhere(action)
-            store_unit(unit)
 
         @pl.when(i == 1)
         def _():
@@ -704,8 +670,7 @@
         def _():
             for hop in (1, 2, 3):
                 norm_to_z(hop).wait_recv()
-            r.norms[0] = (r.norms[4] + r.norms[5]) + (r.norms[6] + r.norms[7])
-            local(r.norms.at[0], r.out_norms, r.store_sem.at[2, 0]).start()
+            r.out_norms[...] = (r.norms[4] + r.norms[5]) + (r.norms[6] + r.norms[7])
 
         return carry
 
@@ -719,8 +684,6 @@
         share_branch(micro).wait_send()
         share_lifted(micro).wait_send()
         share_rest(micro).wait_send()
-        store_result(micro).wait()
-        store_grad(micro).wait()
 
         @pl.when(leading if micro else leading & (c == 1))
         def _():
@@ -746,34 +709,38 @@
 
     lax.fori_loop(0, FAR, drain_far, 0)
 
-    def drain_store(unit, carry):
-        local(r.staged.at[unit], r.out_outward.at[:, 0:COLUMNS], r.unit_sem.at[unit]).wait()
-        return carry
-
-    lax.fori_loop(0, UNITS, drain_store, 0)
-    local(r.norms.at[0], r.out_norms, r.store_sem.at[2, 0]).wait()
-
-
-def hand_over_kernel(*refs):
-    sources, norms, targets = refs[:6], refs[6], refs[7:13]
-    gain_grad, bias_grad, held, in_sem, out_sem = refs[13], refs[14], refs[15:21], refs[21], refs[22]
-    loads = [pltpu.make_async_copy(a, b, in_sem.at[k]) for k, (a, b) in enumerate(zip(sources, held))]
-    stores = [pltpu.make_async_copy(a, b, out_sem.at[k]) for k, (a, b) in enumerate(zip(held, targets))]
-    for load in loads:
-        load.start()
+
+def hand_over_kernel(result, grad, staged, norms, *refs):
+    out_result, out_grad, out_inward, out_outward, out_up, out_down, gain_grad, bias_grad, sem = refs
+    width = result.shape[2]
+
+    def start(source, target):
+        copy = pltpu.make_async_copy(source, target, sem)
+        copy.start()
+        return copy
+
+    copies = [start(result, out_result.at[0, :, 0]), start(grad, out_grad.at[0, :, 0])]
+    for unit in range(UNITS):
+        half = pl.ds(unit % 2 * COLUMNS, COLUMNS)
+        if unit < 8:
+            target = out_down.at[0, pl.ds(unit // 2 * BLOCK, BLOCK), half]
+        elif unit < 16:
+            target = out_up.at[0, :, pl.ds((unit - 8) * COLUMNS, COLUMNS)]
+        elif unit < 18:
+            target = out_outward.at[0, :, half]
+        else:
+            target = out_inward.at[0, :, pl.ds((unit - 18) * COLUMNS, COLUMNS)]
+        copies.append(start(staged.at[unit], target))
     share = gain_grad.shape[2]
-    for index in range(norms.shape[1] // share):
+    for index in range(width // share):
 
         @pl.when(lax.axis_index("dp") == index)
         def _():
             gain_grad[0] = norms[0:2, index * share : (index + 1) * share]
             bias_grad[0] = norms[2:4, index * share : (index + 1) * share]
 
-    for load, store in zip(loads, stores):
-        load.wait()
-        store.start()
-    for store in stores:
-        store.wait()
+    for copy in copies:
+        copy.wait()
 
 
 def step_on_device(
@@ -786,19 +753,16 @@
     in_smem = pl.BlockSpec(memory_space=pltpu.SMEM)
     dma = pltpu.SemaphoreType.DMA
     share = width // lax.axis_size("dp")
-    shapes = [
-        jax.ShapeDtypeStruct((2, length, width), SLIM),
-        jax.ShapeDtypeStruct((2, length, width), WIDE),
-        jax.ShapeDtypeStruct((4 * BLOCK, width), WIDE),
-        jax.ShapeDtypeStruct((BLOCK, wide_ff), WIDE),
-        jax.ShapeDtypeStruct((BLOCK, width), WIDE),
-        jax.ShapeDtypeStruct((BLOCK, 3 * width), WIDE),
-    ]
     made = pl.pallas_call(
         step_kernel,
-        out_shape=(*shapes, jax.ShapeDtypeStruct((8, width), WIDE)),
+        out_shape=(
+            pltpu.VMEM((2, length, width), SLIM),
+            pltpu.VMEM((2, length, width), WIDE),
+            pltpu.VMEM((UNITS, BLOCK, COLUMNS), WIDE),
+            pltpu.VMEM((8, width), WIDE),
+        ),
         in_specs=[anywhere] * 6 + [in_vmem] * 2 + [in_smem] * 2,
-        out_specs=[anywhere] * 7,
+        out_specs=[in_vmem] * 4,
         scratch_shapes=[
             pltpu.VMEM((2, length, width), SLIM),
             pltpu.VMEM((width, 3 * width), SLIM),
@@ -809,12 +773,10 @@
             pltpu.VMEM((7, 8 * BLOCK, 4 * length), SLIM),
             pltpu.VMEM((7, 8 * BLOCK, length), SLIM),
             pltpu.VMEM((2, width // HEAD, length, length), SLIM),
-            pltpu.VMEM((2, length, width), WIDE),
             pltpu.VMEM((length, width), SLIM),
             pltpu.VMEM((length, width), SLIM),
             pltpu.VMEM((width, length), SLIM),
             pltpu.VMEM((length, width), WIDE),
-            pltpu.VMEM((2, length, width), SLIM),
             pltpu.VMEM((2, length, width), SLIM),
             pltpu.VMEM((4, 8, width), WIDE),
             pltpu.VMEM((length, length), WIDE),
@@ -823,37 +785,37 @@
             pltpu.VMEM((NEAR, 5, BLOCK, COLUMNS), SLIM),
             pltpu.VMEM((FAR, BLOCK, COLUMNS), SLIM),
             pltpu.VMEM((FAR, 5, 2, BLOCK, COLUMNS), SLIM),
-            pltpu.VMEM((UNITS, BLOCK, COLUMNS), WIDE),
             pltpu.VMEM((8, 8, width), WIDE),
-            dma((4,)), dma((2,)), dma((3, 2)), dma((UNITS,)),
+            dma((4,)), dma((2,)),
             *[dma((2,))] * 10, pltpu.SemaphoreType.REGULAR,
             dma((NEAR,)), dma((NEAR,)), dma((NEAR, 3)), dma((NEAR, 5)),
             dma((FAR,)), dma((FAR,)), dma((FAR, 3)), dma((FAR, 5)), dma((5,)), dma((5,)),
         ],
         compiler_params=pltpu.CompilerParams(
-            collective_id=0, has_side_effects=True, vmem_limit_bytes=VMEM_BYTES
+            collective_id=0, has_side_effects=True, vmem_limit_bytes=VMEM_BYTES - 4500000
         ),
     )(
         inputs, cotangent, inward_weight, outward_weight, up_weight, down_weight,
         norm_gain, norm_bias, clip_lengths, anchor_offsets,
     )
-    result, grad, down, up, outward, inward, gain_grad, bias_grad = pl.pallas_call(
+    sections = 1
+    return pl.pallas_call(
         hand_over_kernel,
-        out_shape=(*shapes, *[jax.ShapeDtypeStruct((1, 2, share), WIDE)] * 2),
-        in_specs=[anywhere] * 6 + [in_vmem],
+        out_shape=(
+            jax.ShapeDtypeStruct((sections, 2, 1, length, width), SLIM),
+            jax.ShapeDtypeStruct((sections, 2, 1, length, width), WIDE),
+            jax.ShapeDtypeStruct((sections, BLOCK, 3 * width), WIDE),
+            jax.ShapeDtypeStruct((sections, BLOCK, width), WIDE),
+            jax.ShapeDtypeStruct((sections, BLOCK, wide_ff), WIDE),
+            jax.ShapeDtypeStruct((sections, 4 * BLOCK, width), WIDE),
+            jax.ShapeDtypeStruct((sections, 2, share), WIDE),
+            jax.ShapeDtypeStruct((sections, 2, share), WIDE),
+        ),
+        in_specs=[in_vmem] * 4,
         out_specs=[anywhere] * 6 + [in_vmem] * 2,
-        scratch_shapes=[pltpu.VMEM(shape.shape, shape.dtype) for shape in shapes] + [dma((6,)), dma((6,))],
-    )(*made)
-    return (
-        result[None, :, None],
-        grad[None, :, None],
-        inward[None],
-        outward[None],
-        up[None],
-        down[None],
-        gain_grad,
-        bias_grad,
-    )
+        scratch_shapes=[dma],
+        compiler_params=pltpu.CompilerParams(vmem_limit_bytes=1 << 20),
+    )(*[pltpu.with_memory_space_constraint(one, pltpu.VMEM) for one in made])
 
 
 def shifted(x, axis, by):

time: 154 us -> 151 us (0.981)
  Pallas kernels: 153 us -> 150 us
    pallas_call x2, Pallas kernels: 153 us -> 150 us  [the longest x1 148 us: step_on_device(): pl.pallas_call(step_kernel, out_shape=(pltpu.VMEM((2, length, width), SLI...]
where the time goes in v4:
time: 151 us
  Pallas kernels  150 us (99%)
    pallas_call x1, Pallas kernels, step_on_device(): pl.pallas_call(step_kernel, out_shape=(pltpu.VMEM((2, length, width), SLI...  148 us

profile of v4, /device:TPU:0, one launch (start us, length us, event | category | flops | bytes accessed | tf_op | source)
XLA Modules:
  0.0 151.0 jit_solution(7751110854356985757)
XLA Ops:
  0.6 147.7 %shard_map.161 = (bf16[2,256,768]{2,1,0:T(8,128)(2,1)S(1)}, f32[2,256,768]{2,1,0:T(8,128)S(1)}, f32[24,48,384]{2,1,0:T(8,128)S(1)}, f32[8,768]{1,0:T(8,128)S(1)}) custom-call(bf16[2,1,256,768]{3,2,1,0:T(8,128)(2,1)} %refs_0_.1, bf16[2,1,256,768]{3,2,1,0:T(8,128)(2,1)} %refs_1_.1, bf16[1,768,2304]{2,1,0:T(8,128)(2,1)} %refs_2_.1, ...), custom_call_target="tpu_custom_call" | custom-call | tf_op jit(solution)/shard_map/pallas_call | solution.py:756
  148.3 2.5 %shard_map.162 = (bf16[1,2,1,256,768]{4,3,2,1,0:T(8,128)(2,1)}, f32[1,2,1,256,768]{4,3,2,1,0:T(8,128)}, f32[1,48,2304]{2,1,0:T(8,128)}, f32[1,48,768]{2,1,0:T(8,...) custom-call(bf16[2,256,768]{2,1,0:T(8,128)(2,1)S(1)} %get-tuple-element.12.re, ...), custom_call_target="tpu_custom_call" | custom-call | tf_op jit(solution)/shard_map/pallas_call | solution.py:802

commit v5 on v4

--- a/solution.py
+++ b/solution.py
@@ -20,14 +20,25 @@
 NEAR = UNITS - FAR
 BLOCK = 48
 COLUMNS = 384
-EARLY_NEAR = 4
+EARLY_NEAR = 5
 HOLD = 1
-LAGS = (2, 3, 4)
-FAR_AT = (-1, -1, 3, 8)
-FAR_FIRST = (2, 4, 10, 15)
-FAR_SECOND = (5, 15, 14, 20)
-FAR_ARRIVED = (17, 18, 20, 21)
-FAR_DONE = (20, 21, 22, 23)
+LAGS = (3, 6, 8)
+FAR_AT = (-1, -1, -1, 6)
+FAR_FIRST = (2, 5, 10, 11)
+FAR_SECOND = (6, 11, 16, 14)
+FAR_ARRIVED = (17, 20, 21, 19)
+FAR_DONE = (22, 27, 24, 21)
+EARLY_FAR = sum(step < 0 for step in FAR_AT)
+
+
+PIECES = [s if s < EARLY_FAR else 8 + s - EARLY_FAR for s in range(FAR)]
+PIECES += [s - FAR + EARLY_FAR if s - FAR < 8 - EARLY_FAR else s for s in range(FAR, UNITS)]
+
+
+def piece_of(slot):
+    near = slot - FAR
+    far_piece = jnp.where(slot < EARLY_FAR, slot, 8 + slot - EARLY_FAR)
+    return jnp.where(slot < FAR, far_piece, jnp.where(near < 8 - EARLY_FAR, near + EARLY_FAR, slot))
 
 
 def times(left, right):
@@ -151,21 +162,18 @@
     r.normed[...] = norm_rows_bf16(r, r.middle[micro], 1)
     r.turned[...] = r.normed[...].T
     place(r, 4, tokens)
-    r.total[...] = r.middle[micro]
 
     @pl.when(first)
     def _():
         r.load_up.wait()
         r.load_down.wait()
 
-    for part in range(4):
-        cols = slice(part * width, (part + 1) * width)
-        lifted = times(r.normed[...], r.up[:, cols])
+    def activate(part):
+        lifted = times(r.normed[...], r.up[:, part * width : (part + 1) * width])
         cumulative = 0.5 * (1.0 + lax.erf(lifted * 0.7071067811865476))
         density = jnp.exp(-0.5 * lifted * lifted) * 0.3989422804014327
         r.grads[1 + part, tokens, :] = (cumulative + lifted * density).astype(SLIM)
         active = (lifted * cumulative).astype(SLIM)
-        r.total[...] += times(active, r.down[cols, :])
         r.turned[...] = active.T
         for y in range(2):
             for piece in range(4):
@@ -175,6 +183,44 @@
                 other = pl.ds(pl.multiple_of(start + (1 - r.c) * 192, 16), BLOCK)
                 r.acts[piece, rows, tokens] = r.turned[own, :]
                 r.acts_out[piece, rows, :] = r.turned[other, :]
+        return active
+
+    @pl.when(leading)
+    def _():
+        r.total[...] = r.middle[micro]
+        for part in range(4):
+            r.total[...] += times(activate(part), r.down[part * width : (part + 1) * width, :])
+        r.result[micro] = r.total[...].astype(SLIM)
+
+    @pl.when(jnp.logical_not(leading))
+    def _():
+        for part in range(4):
+            set_aside(r, micro * 12 + 2 * part, activate(part))
+        middle = r.middle[micro]
+        upper = middle.astype(SLIM)
+        set_aside(r, micro * 12 + 8, upper)
+        set_aside(r, micro * 12 + 10, (middle - upper.astype(WIDE)).astype(SLIM))
+
+
+def set_aside(r, slot, values):
+    for half in range(2):
+        columns = values[:, half * COLUMNS : (half + 1) * COLUMNS]
+        r.partial[slot + half, 0] = columns[:192]
+        r.partial[slot + half, 1, 0:64] = columns[192:]
+
+
+def set_back(r, slot):
+    halves = [
+        jnp.concatenate([r.partial[slot + half, 0], r.partial[slot + half, 1, 0:64]], 0) for half in range(2)
+    ]
+    return jnp.concatenate(halves, 1)
+
+
+def last_output(r, micro):
+    width = r.normed.shape[1]
+    r.total[...] = set_back(r, micro * 12 + 8).astype(WIDE) + set_back(r, micro * 12 + 10).astype(WIDE)
+    for part in range(4):
+        r.total[...] += times(set_back(r, micro * 12 + 2 * part), r.down[part * width : (part + 1) * width, :])
     r.result[micro] = r.total[...].astype(SLIM)
 
 
@@ -372,9 +418,10 @@
         share_branch(micro).start()
 
     def weight_operands(unit):
-        whole = lax.div(unit, 2)
+        piece = piece_of(unit)
+        whole = lax.div(piece, 2)
         slab = jnp.minimum(whole, 4) + jnp.where(whole >= 8, 1, 0) + jnp.where(whole >= 9, 1, 0)
-        cols = pl.ds(pl.multiple_of(lax.rem(unit, 2) * COLUMNS, 128), COLUMNS)
+        cols = pl.ds(pl.multiple_of(lax.rem(piece, 2) * COLUMNS, 128), COLUMNS)
         other = pl.ds(pl.multiple_of((1 - y) * 192, 64), 192)
         own = pl.ds(pl.multiple_of(y * 192, 64), 192)
         return slab, other, own, r.grads[jnp.maximum(whole - 3, 0), :, cols]
@@ -486,21 +533,24 @@
             def _():
                 everyone_in()
 
+            ahead = leading & (c == 0) & (t == 0)
+
+            @pl.when(ahead)
+            def _():
+                relay_up(0).start()
+                relay_up(0).wait_send()
+                pl.semaphore_signal(r.turn, inc=1, device_id=(section, pair_dp), device_id_type=MESH)
+
+            @pl.when(leading & (t == 1))
+            def _():
+                relay_up(1).start()
+
             share_acts(micro).start()
-            ahead = leading & (c == 0) & (t == 0)
 
             @pl.when(leading & (c == 1) & (t == 0))
             def _():
                 pl.semaphore_wait(r.turn, 1)
-
-            @pl.when(leading)
-            def _():
-                relay_up(micro).start()
-
-            @pl.when(ahead)
-            def _():
-                relay_up(0).wait_send()
-                pl.semaphore_signal(r.turn, inc=1, device_id=(section, pair_dp), device_id_type=MESH)
+                relay_up(0).start()
 
         @pl.when(leading & (t == 3))
         def _():
@@ -517,6 +567,14 @@
 
             share_rest(micro).start()
 
+            @pl.when(trailing & (t == 4))
+            def _():
+                def body(done, carry):
+                    last_output(r, done)
+                    return carry
+
+                lax.fori_loop(0, 2, body, 0)
+
         @pl.when(leading & (t == 4))
         def _():
             arrive(1)
@@ -526,21 +584,19 @@
             for micro in range(2):
                 share_branch(micro, 1 - c).wait_recv()
                 share_acts(micro, 1 - c).wait_recv()
-
-            early_far = sum(at < 0 for at in FAR_AT)
 
             def body(i, carry):
                 @pl.when(i < EARLY_NEAR)
                 def _():
                     near_unit(FAR + i)
 
-                @pl.when(i < early_far)
+                @pl.when(i < EARLY_FAR)
                 def _():
                     far_unit(i)
 
                 return carry
 
-            lax.fori_loop(0, max(EARLY_NEAR, early_far), body, 0)
+            lax.fori_loop(0, max(EARLY_NEAR, EARLY_FAR), body, 0)
 
         return carry
 
@@ -579,6 +635,11 @@
         return (i >= lag) & (i < NEAR + lag), jnp.clip(i - lag, 0, NEAR - 1) + FAR
 
     def advance(i, carry):
+        @pl.when(i < NEAR)
+        def _():
+            sum_y(FAR + i)
+            at_ends(FAR + i, near_z, r.z_in)
+
         issued = FAR + EARLY_NEAR + i - HOLD
 
         @pl.when(issued == 16)
@@ -595,11 +656,6 @@
         @pl.when(turn)
         def _(unit=unit):
             far_unit(unit)
-
-        @pl.when(i < NEAR)
-        def _():
-            sum_y(FAR + i)
-            at_ends(FAR + i, near_z, r.z_in)
 
         turn, unit = near_turn(i, LAGS[0])
 
@@ -674,7 +730,7 @@
 
         return carry
 
-    lax.fori_loop(0, max(NEAR + LAGS[2], FAR_DONE[-1] + 1), advance, 0)
+    lax.fori_loop(0, max(NEAR + LAGS[2], *(step + 1 for step in FAR_DONE)), advance, 0)
 
     norm_to_y().wait_send()
     for hop in (1, 2, 3):
@@ -720,17 +776,17 @@
         return copy
 
     copies = [start(result, out_result.at[0, :, 0]), start(grad, out_grad.at[0, :, 0])]
-    for unit in range(UNITS):
-        half = pl.ds(unit % 2 * COLUMNS, COLUMNS)
-        if unit < 8:
-            target = out_down.at[0, pl.ds(unit // 2 * BLOCK, BLOCK), half]
-        elif unit < 16:
-            target = out_up.at[0, :, pl.ds((unit - 8) * COLUMNS, COLUMNS)]
-        elif unit < 18:
+    for slot, piece in enumerate(PIECES):
+        half = pl.ds(piece % 2 * COLUMNS, COLUMNS)
+        if piece < 8:
+            target = out_down.at[0, pl.ds(piece // 2 * BLOCK, BLOCK), half]
+        elif piece < 16:
+            target = out_up.at[0, :, pl.ds((piece - 8) * COLUMNS, COLUMNS)]
+        elif piece < 18:
             target = out_outward.at[0, :, half]
         else:
-            target = out_inward.at[0, :, pl.ds((unit - 18) * COLUMNS, COLUMNS)]
-        copies.append(start(staged.at[unit], target))
+            target = out_inward.at[0, :, pl.ds((piece - 18) * COLUMNS, COLUMNS)]
+        copies.append(start(staged.at[slot], target))
     share = gain_grad.shape[2]
     for index in range(width // share):
 

time: 151 us -> 149 us (0.987)
  Pallas kernels: 150 us -> 148 us
    pallas_call x1, Pallas kernels: 148 us -> 145 us  [step_on_device(): pl.pallas_call(step_kernel, out_shape=(pltpu.VMEM((2, length, width), SLI...]
where the time goes in v5:
time: 149 us; the launch traced here: 148 us
  Pallas kernels  148 us (99%)
    pallas_call x1, Pallas kernels, step_on_device(): pl.pallas_call(step_kernel, out_shape=(pltpu.VMEM((2, length, width), SLI...  145 us

profile of v5, /device:TPU:0, one launch (start us, length us, event | category | flops | bytes accessed | tf_op | source)
XLA Modules:
  0.0 148.5 jit_solution(2931970643276329343)
XLA Ops:
  0.6 145.2 %shard_map.161 = (bf16[2,256,768]{2,1,0:T(8,128)(2,1)S(1)}, f32[2,256,768]{2,1,0:T(8,128)S(1)}, f32[24,48,384]{2,1,0:T(8,128)S(1)}, f32[8,768]{1,0:T(8,128)S(1)}) custom-call(bf16[2,1,256,768]{3,2,1,0:T(8,128)(2,1)} %refs_0_.1, bf16[2,1,256,768]{3,2,1,0:T(8,128)(2,1)} %refs_1_.1, bf16[1,768,2304]{2,1,0:T(8,128)(2,1)} %refs_2_.1, ...), custom_call_target="tpu_custom_call" | custom-call | tf_op jit(solution)/shard_map/pallas_call | solution.py:812
  145.8 2.5 %shard_map.162 = (bf16[1,2,1,256,768]{4,3,2,1,0:T(8,128)(2,1)}, f32[1,2,1,256,768]{4,3,2,1,0:T(8,128)}, f32[1,48,2304]{2,1,0:T(8,128)}, f32[1,48,768]{2,1,0:T(8,...) custom-call(bf16[2,256,768]{2,1,0:T(8,128)(2,1)S(1)} %get-tuple-element.12.re, ...), custom_call_target="tpu_custom_call" | custom-call | tf_op jit(solution)/shard_map/pallas_call | solution.py:858

commit v6 on v5

--- a/solution.py
+++ b/solution.py
@@ -16,29 +16,22 @@
 VMEM_BYTES = 67043328
 
 UNITS = 24
-FAR = 4
-NEAR = UNITS - FAR
+FAR = 2
+QUAD = 8
+NEAR = UNITS - QUAD
 BLOCK = 48
 COLUMNS = 384
-EARLY_NEAR = 5
-HOLD = 1
-LAGS = (3, 6, 8)
-FAR_AT = (-1, -1, -1, 6)
-FAR_FIRST = (2, 5, 10, 11)
-FAR_SECOND = (6, 11, 16, 14)
-FAR_ARRIVED = (17, 20, 21, 19)
-FAR_DONE = (22, 27, 24, 21)
-EARLY_FAR = sum(step < 0 for step in FAR_AT)
-
-
-PIECES = [s if s < EARLY_FAR else 8 + s - EARLY_FAR for s in range(FAR)]
-PIECES += [s - FAR + EARLY_FAR if s - FAR < 8 - EARLY_FAR else s for s in range(FAR, UNITS)]
-
-
-def piece_of(slot):
-    near = slot - FAR
-    far_piece = jnp.where(slot < EARLY_FAR, slot, 8 + slot - EARLY_FAR)
-    return jnp.where(slot < FAR, far_piece, jnp.where(near < 8 - EARLY_FAR, near + EARLY_FAR, slot))
+EARLY_NEAR = 2
+HOLD = 0
+LAGS = (2, 4, 6)
+FAR_FIRST = (0, 5)
+FAR_SECOND = (2, 9)
+FAR_ARRIVED = (3, 18)
+FAR_DONE = (7, 21)
+QUAD_AT = (-1, -1, 2, 4, 6, 12)
+QUAD_FIRST = (3, 2, 6, 7, 9, 13)
+QUAD_SECOND = (5, 7, 15, 13, 11, 16)
+QUAD_DONE = (18, 13, 19, 21, 12, 20)
 
 
 def times(left, right):
@@ -125,7 +118,7 @@
             r.load_rest()
 
     for part in range(3):
-        r.grads[6 + part, tokens, :] = times(
+        r.grads[5 + part, tokens, :] = times(
             r.normed[...], r.inward[:, part * width : (part + 1) * width]
         ).astype(SLIM)
 
@@ -134,13 +127,13 @@
         r.share_acts(0).wait_send()
 
     r.turned[...] = r.normed[...].T
-    place(r, 6, tokens)
+    place(r, 3, tokens)
     one, two = (lanes.astype(SLIM) for lanes in head_lanes())
     for pair in range(width // (2 * HEAD)):
         cols = pl.ds(pair * 2 * HEAD, 2 * HEAD)
-        queries = r.grads[6, tokens, cols] * jnp.asarray(HEAD**-0.5, SLIM)
-        keys = r.grads[7, tokens, cols]
-        values_turned = r.grads[8, tokens, cols].T
+        queries = r.grads[5, tokens, cols] * jnp.asarray(HEAD**-0.5, SLIM)
+        keys = r.grads[6, tokens, cols]
+        values_turned = r.grads[7, tokens, cols].T
         scores = times_turned(jnp.concatenate([keys * one, keys * two], 0), queries)
         pieces = []
         for head in range(2):
@@ -152,7 +145,7 @@
         attended_turned = jnp.concatenate(pieces, 0)
         r.turned[cols, :] = attended_turned
         r.held[:, cols] = attended_turned.T
-    place(r, 5, tokens)
+    place(r, 2, tokens)
 
     @pl.when(first)
     def _():
@@ -161,7 +154,7 @@
     r.middle[micro] = r.stream[micro].astype(WIDE) + times(r.held[...], r.outward[...])
     r.normed[...] = norm_rows_bf16(r, r.middle[micro], 1)
     r.turned[...] = r.normed[...].T
-    place(r, 4, tokens)
+    place(r, 1, tokens)
 
     @pl.when(first)
     def _():
@@ -172,17 +165,26 @@
         lifted = times(r.normed[...], r.up[:, part * width : (part + 1) * width])
         cumulative = 0.5 * (1.0 + lax.erf(lifted * 0.7071067811865476))
         density = jnp.exp(-0.5 * lifted * lifted) * 0.3989422804014327
-        r.grads[1 + part, tokens, :] = (cumulative + lifted * density).astype(SLIM)
+        r.grads[part, tokens, :] = (cumulative + lifted * density).astype(SLIM)
         active = (lifted * cumulative).astype(SLIM)
         r.turned[...] = active.T
+        rows = pl.ds(part * BLOCK, BLOCK)
         for y in range(2):
-            for piece in range(4):
-                rows = pl.ds(y * 192 + part * BLOCK, BLOCK)
-                start = 384 * y + BLOCK * piece
-                own = pl.ds(pl.multiple_of(start + r.c * 192, 16), BLOCK)
-                other = pl.ds(pl.multiple_of(start + (1 - r.c) * 192, 16), BLOCK)
-                r.acts[piece, rows, tokens] = r.turned[own, :]
-                r.acts_out[piece, rows, :] = r.turned[other, :]
+            placed = pl.ds(y * 192 + part * BLOCK, BLOCK)
+            own = pl.ds(pl.multiple_of(384 * y + r.c * 192, 16), BLOCK)
+            other = pl.ds(pl.multiple_of(384 * y + (1 - r.c) * 192, 16), BLOCK)
+            r.acts[0, placed, tokens] = r.turned[own, :]
+            r.acts_out[0, placed, :] = r.turned[other, :]
+        for piece in range(3):
+
+            def rows_for(core, side):
+                start = 384 * side + 192 * core + BLOCK * (piece + 1)
+                return r.turned[pl.ds(pl.multiple_of(start, 16), BLOCK), :]
+
+            r.quad_acts[piece, rows, r.quad_rows(micro)] = rows_for(r.c, r.y)
+            r.quad_out[micro, 0, piece, rows, :] = rows_for(1 - r.c, r.y)
+            r.quad_out[micro, 1, piece, rows, :] = rows_for(r.c, 1 - r.y)
+            r.quad_out[micro, 2, piece, rows, :] = rows_for(1 - r.c, 1 - r.y)
         return active
 
     @pl.when(leading)
@@ -230,25 +232,25 @@
     r.total[...] = jnp.zeros((length, width), WIDE)
     for part in range(4):
         cols = slice(part * width, (part + 1) * width)
-        hidden = times_turned(r.grads[0, tokens, :], r.down[cols, :])
-        lifted_grad = (hidden * r.grads[1 + part, tokens, :].astype(WIDE)).astype(SLIM)
-        r.grads[1 + part, tokens, :] = lifted_grad
+        hidden = times_turned(r.branch[r.quad_rows(micro), :], r.down[cols, :])
+        lifted_grad = (hidden * r.grads[part, tokens, :].astype(WIDE)).astype(SLIM)
+        r.grads[part, tokens, :] = lifted_grad
         r.total[...] += times_turned(lifted_grad, r.up[:, cols])
     r.share_lifted(micro).start()
-    middle_grad = r.grads[0, tokens, :].astype(WIDE) + norm_backward(
+    middle_grad = r.branch[r.quad_rows(micro), :].astype(WIDE) + norm_backward(
         r, r.middle[micro], r.total[...], 1
     )
     r.middle[micro] = middle_grad
-    r.grads[5, tokens, :] = middle_grad.astype(SLIM)
-    r.held[...] = times_turned(r.grads[5, tokens, :], r.outward[...]).astype(SLIM)
+    r.grads[4, tokens, :] = middle_grad.astype(SLIM)
+    r.held[...] = times_turned(r.grads[4, tokens, :], r.outward[...]).astype(SLIM)
     first, second = head_lanes()
     one, two = first.astype(SLIM), second.astype(SLIM)
     scaling = HEAD**-0.5
     for pair in range(width // (2 * HEAD)):
         cols = pl.ds(pair * 2 * HEAD, 2 * HEAD)
-        queries = r.grads[6, tokens, cols] * jnp.asarray(scaling, SLIM)
-        values = r.grads[8, tokens, cols]
-        keys_turned = r.grads[7, tokens, cols].T
+        queries = r.grads[5, tokens, cols] * jnp.asarray(scaling, SLIM)
+        values = r.grads[7, tokens, cols]
+        keys_turned = r.grads[6, tokens, cols].T
         incoming = r.held[:, cols]
         weight_grads = times_turned(jnp.concatenate([values * one, values * two], 0), incoming)
         score_grads, query_grads, weights = [], [], []
@@ -264,26 +266,27 @@
             )
         key_grad = times(jnp.concatenate(score_grads, 0), queries)
         value_grad = times(jnp.concatenate(weights, 0), incoming)
-        r.grads[6, tokens, cols] = jnp.concatenate(query_grads, 0).T
-        r.grads[7, tokens, cols] = (key_grad[:length] * first + key_grad[length:] * second).astype(SLIM)
-        r.grads[8, tokens, cols] = (value_grad[:length] * first + value_grad[length:] * second).astype(SLIM)
-    norm_grad = times_turned(r.grads[6, tokens, :], r.inward[:, 0:width])
+        r.grads[5, tokens, cols] = jnp.concatenate(query_grads, 0).T
+        r.grads[6, tokens, cols] = (key_grad[:length] * first + key_grad[length:] * second).astype(SLIM)
+        r.grads[7, tokens, cols] = (value_grad[:length] * first + value_grad[length:] * second).astype(SLIM)
+    norm_grad = times_turned(r.grads[5, tokens, :], r.inward[:, 0:width])
     for part in range(1, 3):
-        norm_grad += times_turned(r.grads[6 + part, tokens, :], r.inward[:, part * width : (part + 1) * width])
+        norm_grad += times_turned(r.grads[5 + part, tokens, :], r.inward[:, part * width : (part + 1) * width])
     r.total[...] = norm_grad
     input_grad = r.middle[micro] + norm_backward(r, r.stream[micro].astype(WIDE), r.total[...], 0)
     r.middle[micro] = input_grad
-    r.passed[micro] = input_grad.astype(SLIM)
+    r.stream[micro] = input_grad.astype(SLIM)
 
 
 NAMES = (
     "x_in", "cot_in", "inward_in", "outward_in", "up_in", "down_in", "gain", "bias", "lengths", "offsets",
     "result", "middle", "staged", "out_norms",
-    "stream", "inward", "outward", "up", "down", "grads", "acts", "acts_out", "weights", "normed", "held",
-    "turned", "total", "passed", "sums", "bias_mask",
+    "stream", "inward", "outward", "up", "down", "grads", "branch", "acts", "acts_out", "quad_acts", "quad_out", "weights", "normed", "held",
+    "turned", "total", "sums", "bias_mask",
     "partial", "y_in", "z_in", "far_y_in", "far_z_in", "norms",
     "load_sem", "source_sem",
     "relay_send", "relay_recv", "acts_send", "acts_recv", "branch_send", "branch_recv", "lifted_send", "lifted_recv",
+    "across_send", "across_recv", "onward_send", "onward_recv", "quad_send", "quad_recv",
     "rest_send", "rest_recv", "turn",
     "y_send", "y_recv", "z_send", "z_recv", "far_y_send", "far_y_recv", "far_z_send", "far_z_recv", "norm_send", "norm_recv",
 )
@@ -293,13 +296,19 @@
     r = types.SimpleNamespace(**dict(zip(NAMES, refs)))
     section, dp = lax.axis_index("section"), lax.axis_index("dp")
     c, y, z = lax.rem(dp, 2), lax.rem(lax.div(dp, 2), 2), lax.div(dp, 4)
-    r.c = c
+    r.c, r.y = c, y
     length = r.normed.shape[0]
     leading = section == 0
     pair_dp, y_dp = dp + 1 - 2 * c, dp + 2 - 4 * y
+    diagonal_dp = pair_dp + y_dp - dp
 
     def slot_of(core, micro):
         return pl.ds(pl.multiple_of((core * 2 + micro) * length, length), length)
+
+    def quad_rows(micro, core=c, side=y):
+        return pl.ds(pl.multiple_of(((side * 2 + core) * 2 + micro) * length, length), length)
+
+    r.quad_rows = quad_rows
 
     def remote(src, dst, send, recv, to_section, to_dp):
         return pltpu.make_async_remote_copy(
@@ -326,14 +335,14 @@
         return local(r.x_in.at[micro, 0], r.stream.at[micro], r.source_sem.at[micro])
 
     def load_cot(micro):
-        return local(r.cot_in.at[micro, 0], r.grads.at[0, slot_of(c, micro)], r.source_sem.at[micro])
+        return local(r.cot_in.at[micro, 0], r.branch.at[quad_rows(micro)], r.source_sem.at[micro])
 
     def relay_up(micro):
         return remote(r.result.at[micro], r.stream.at[micro], r.relay_send.at[micro], r.relay_recv.at[micro], 1 - section, dp)
 
     def relay_back(micro):
         return remote(
-            r.passed.at[micro], r.grads.at[0, slot_of(c, micro)], r.relay_send.at[micro], r.relay_recv.at[micro], 1 - section, dp
+            r.stream.at[micro], r.branch.at[quad_rows(micro)], r.relay_send.at[micro], r.relay_recv.at[micro], 1 - section, dp
         )
 
     def share_acts(micro, core=c):
@@ -341,20 +350,37 @@
             r.acts_out, r.acts.at[:, :, slot_of(core, micro)], r.acts_send.at[micro], r.acts_recv.at[micro], section, pair_dp
         )
 
+    def branch_copy(rows, send, recv, to_dp):
+        return remote(r.branch.at[rows], r.branch.at[rows], send, recv, section, to_dp)
+
     def share_branch(micro, core=c):
-        rows = slot_of(core, micro)
-        return remote(r.grads.at[0, rows], r.grads.at[0, rows], r.branch_send.at[micro], r.branch_recv.at[micro], section, pair_dp)
+        return branch_copy(quad_rows(micro, core), r.branch_send.at[micro], r.branch_recv.at[micro], pair_dp)
+
+    def branch_across(micro, side=y):
+        return branch_copy(quad_rows(micro, c, side), r.across_send.at[micro], r.across_recv.at[micro], y_dp)
+
+    def branch_onward(micro, core=c):
+        return branch_copy(quad_rows(micro, core, 1 - y), r.onward_send.at[micro], r.onward_recv.at[micro], pair_dp)
+
+    def share_quad(micro, peer, arriving=False):
+        to_dp = (pair_dp, y_dp, diagonal_dp)[peer]
+        core = 1 - c if arriving and peer != 1 else c
+        side = 1 - y if arriving and peer != 0 else y
+        return remote(
+            r.quad_out.at[micro, peer], r.quad_acts.at[:, :, quad_rows(micro, core, side)],
+            r.quad_send.at[micro, peer], r.quad_recv.at[micro, peer], section, to_dp,
+        )
 
     def share_lifted(micro, core=c):
         rows = slot_of(core, micro)
         return remote(
-            r.grads.at[1:5, rows], r.grads.at[1:5, rows], r.lifted_send.at[micro], r.lifted_recv.at[micro], section, pair_dp
+            r.grads.at[0:4, rows], r.grads.at[0:4, rows], r.lifted_send.at[micro], r.lifted_recv.at[micro], section, pair_dp
         )
 
     def share_rest(micro, core=c):
         rows = slot_of(core, micro)
         return remote(
-            r.grads.at[5:9, rows], r.grads.at[5:9, rows], r.rest_send.at[micro], r.rest_recv.at[micro], section, pair_dp
+            r.grads.at[4:8, rows], r.grads.at[4:8, rows], r.rest_send.at[micro], r.rest_recv.at[micro], section, pair_dp
         )
 
     r.share_lifted = share_lifted
@@ -362,7 +388,7 @@
 
     def to_y(unit):
         return remote(
-            r.partial.at[unit, 0], r.y_in.at[unit - FAR], r.y_send.at[unit - FAR], r.y_recv.at[unit - FAR], section, y_dp
+            r.partial.at[unit, 0], r.y_in.at[unit - QUAD], r.y_send.at[unit - QUAD], r.y_recv.at[unit - QUAD], section, y_dp
         )
 
     def rows_of(place):
@@ -406,6 +432,7 @@
 
     barrier = pltpu.get_barrier_semaphore()
     peers = [(1 - section, dp), (section, pair_dp), (section, y_dp)]
+    peers += [(section, diagonal_dp)]
     peers += [(section, lax.rem(dp + 4 * hop, 16)) for hop in (1, 2, 3)]
     for peer in peers:
         pl.semaphore_signal(barrier, inc=1, device_id=peer, device_id_type=MESH)
@@ -415,28 +442,33 @@
 
     def arrive(micro):
         relay_back(micro).wait_recv()
+        branch_across(micro).start()
         share_branch(micro).start()
 
-    def weight_operands(unit):
-        piece = piece_of(unit)
-        whole = lax.div(piece, 2)
-        slab = jnp.minimum(whole, 4) + jnp.where(whole >= 8, 1, 0) + jnp.where(whole >= 9, 1, 0)
-        cols = pl.ds(pl.multiple_of(lax.rem(piece, 2) * COLUMNS, 128), COLUMNS)
-        other = pl.ds(pl.multiple_of((1 - y) * 192, 64), 192)
-        own = pl.ds(pl.multiple_of(y * 192, 64), 192)
-        return slab, other, own, r.grads[jnp.maximum(whole - 3, 0), :, cols]
+    def columns_of(unit):
+        return pl.ds(pl.multiple_of(lax.rem(unit, 2) * COLUMNS, 128), COLUMNS)
+
+    def side_rows(side):
+        return pl.ds(pl.multiple_of(side * 192, 64), 192)
 
     def near_unit(unit):
-        slab, other, own, grads = weight_operands(unit)
-        r.partial[unit, 0] = times(r.acts[slab, other, :], grads).astype(SLIM)
+        whole = lax.div(unit, 2)
+        slab = 1 + jnp.where(whole >= 8, 1, 0) + jnp.where(whole >= 9, 1, 0)
+        grads = r.grads[whole - 4, :, columns_of(unit)]
+        r.partial[unit, 0] = times(r.acts[slab, side_rows(1 - y), :], grads).astype(SLIM)
         to_y(unit).start()
-        r.partial[unit, 1] = times(r.acts[slab, own, :], grads).astype(SLIM)
+        r.partial[unit, 1] = times(r.acts[slab, side_rows(y), :], grads).astype(SLIM)
 
     def far_unit(unit):
-        slab, other, own, grads = weight_operands(unit)
-        r.partial[unit, 0] = times(r.acts[slab, other, :], grads).astype(SLIM)
-        r.partial[unit, 1] = times(r.acts[slab, own, :], grads).astype(SLIM)
+        grads = r.branch[pl.ds(pl.multiple_of(y * 4 * length, length), 4 * length), columns_of(unit)]
+        r.partial[unit, 0] = times(r.acts[0, side_rows(1 - y), :], grads).astype(SLIM)
+        r.partial[unit, 1] = times(r.acts[0, side_rows(y), :], grads).astype(SLIM)
         at_ends(unit, far_z, r.far_z_in)
+
+    def quad_unit(unit):
+        grads = r.branch[:, columns_of(unit)]
+        r.partial[unit, 1] = times(r.quad_acts[lax.div(unit, 2) - 1], grads).astype(SLIM)
+        at_ends(unit, near_z, r.z_in)
 
     def arrived(unit, index, copy, into):
         copy(unit, 0, index, 0, dp).wait_recv()
@@ -513,6 +545,7 @@
             everyone_in()
             for micro in range(2):
                 load_cot(micro).wait()
+                branch_across(micro).start()
                 share_branch(micro).start()
 
         @pl.when(is_forward)
@@ -552,6 +585,9 @@
                 pl.semaphore_wait(r.turn, 1)
                 relay_up(0).start()
 
+            for peer in range(3):
+                share_quad(micro, peer).start()
+
         @pl.when(leading & (t == 3))
         def _():
             arrive(0)
@@ -585,18 +621,11 @@
                 share_branch(micro, 1 - c).wait_recv()
                 share_acts(micro, 1 - c).wait_recv()
 
-            def body(i, carry):
-                @pl.when(i < EARLY_NEAR)
-                def _():
-                    near_unit(FAR + i)
-
-                @pl.when(i < EARLY_FAR)
-                def _():
-                    far_unit(i)
-
+            def body(unit, carry):
+                far_unit(unit)
                 return carry
 
-            lax.fori_loop(0, max(EARLY_NEAR, EARLY_FAR), body, 0)
+            lax.fori_loop(0, FAR, body, 0)
 
         return carry
 
@@ -619,43 +648,68 @@
     for micro in range(2):
         share_lifted(micro, 1 - c).wait_recv()
 
+    def early_near(ahead, carry):
+        near_unit(QUAD + ahead)
+        return carry
+
+    lax.fori_loop(0, EARLY_NEAR, early_near, 0)
+    for micro in range(2):
+        branch_across(micro, 1 - y).wait_recv()
+        branch_onward(micro).start()
+    for micro in range(2):
+        branch_onward(micro, 1 - c).wait_recv()
+        for peer in range(3):
+            share_quad(micro, peer, True).wait_recv()
+
+    def early_quad(unit, carry):
+        quad_unit(unit)
+        return carry
+
+    lax.fori_loop(FAR, FAR + sum(step < 0 for step in QUAD_AT), early_quad, 0)
+
     def sum_y(unit):
         to_y(unit).wait_recv()
-        r.partial[unit, 1] = (r.partial[unit, 1].astype(WIDE) + r.y_in[unit - FAR].astype(WIDE)).astype(SLIM)
-
-    def far_turn(i, steps):
-        turn, unit = i < 0, jnp.int32(0)
+        r.partial[unit, 1] = (r.partial[unit, 1].astype(WIDE) + r.y_in[unit - QUAD].astype(WIDE)).astype(SLIM)
+
+    def turn_of(i, steps, base):
+        turn, unit = i < 0, jnp.int32(base)
         for index, step in enumerate(steps):
             if step >= 0:
                 turn = turn | (i == step)
-                unit = jnp.where(i == step, index, unit)
+                unit = jnp.where(i == step, base + index, unit)
         return turn, unit
 
     def near_turn(i, lag):
-        return (i >= lag) & (i < NEAR + lag), jnp.clip(i - lag, 0, NEAR - 1) + FAR
+        return (i >= lag) & (i < NEAR + lag), jnp.clip(i - lag, 0, NEAR - 1) + QUAD
+
+    def end_of_line(unit):
+        def action(here):
+            r.staged[unit] = gathered(unit, here, near_z, r.z_in)
+
+        everywhere(action)
 
     def advance(i, carry):
-        @pl.when(i < NEAR)
-        def _():
-            sum_y(FAR + i)
-            at_ends(FAR + i, near_z, r.z_in)
-
-        issued = FAR + EARLY_NEAR + i - HOLD
+        issued = QUAD + EARLY_NEAR + i - HOLD
 
         @pl.when(issued == 16)
         def _():
             for micro in range(2):
                 share_rest(micro, 1 - c).wait_recv()
 
-        @pl.when((issued >= FAR + EARLY_NEAR) & (issued < UNITS))
+        @pl.when((issued >= QUAD + EARLY_NEAR) & (issued < UNITS))
         def _():
             near_unit(issued)
 
-        turn, unit = far_turn(i, FAR_AT)
+        @pl.when(i < NEAR)
+        def _():
+            sum_y(QUAD + i)
+            at_ends(QUAD + i, near_z, r.z_in)
+
+        turn, unit = turn_of(i, QUAD_AT, FAR)
 
         @pl.when(turn)
         def _(unit=unit):
-            far_unit(unit)
+            quad_unit(unit)
 
         turn, unit = near_turn(i, LAGS[0])
 
@@ -663,19 +717,49 @@
         def _(unit=unit):
             at_middle_first(unit, near_z, r.z_in)
 
-        turn, unit = far_turn(i, FAR_FIRST)
+        turn, unit = turn_of(i, FAR_FIRST, 0)
 
         @pl.when(turn)
         def _(unit=unit):
             at_middle_first(unit, far_z, r.far_z_in)
 
-        turn, unit = far_turn(i, FAR_SECOND)
+        turn, unit = turn_of(i, QUAD_FIRST, FAR)
+
+        @pl.when(turn)
+        def _(unit=unit):
+            at_middle_first(unit, near_z, r.z_in)
+
+        turn, unit = turn_of(i, FAR_SECOND, 0)
 
         @pl.when(turn)
         def _(unit=unit):
             at_middle_second(unit, far_z, r.far_z_in)
 
-        turn, unit = far_turn(i, FAR_ARRIVED)
+        turn, unit = turn_of(i, QUAD_SECOND, FAR)
+
+        @pl.when(turn)
+        def _(unit=unit):
+            at_middle_second(unit, near_z, r.z_in)
+
+        turn, unit = near_turn(i, LAGS[1])
+
+        @pl.when(turn)
+        def _(unit=unit):
+            at_middle_second(unit, near_z, r.z_in)
+
+        turn, unit = turn_of(i, QUAD_DONE, FAR)
+
+        @pl.when(turn)
+        def _(unit=unit):
+            end_of_line(unit)
+
+        turn, unit = near_turn(i, LAGS[2])
+
+        @pl.when(turn)
+        def _(unit=unit):
+            end_of_line(unit)
+
+        turn, unit = turn_of(i, FAR_ARRIVED, 0)
 
         @pl.when(turn)
         def _(unit=unit):
@@ -687,28 +771,13 @@
 
             everywhere(action)
 
-        turn, unit = far_turn(i, FAR_DONE)
+        turn, unit = turn_of(i, FAR_DONE, 0)
 
         @pl.when(turn)
         def _(unit=unit):
             far_to_y(unit, 0).wait_recv()
             r.staged[unit] += r.far_y_in[unit].astype(WIDE)
 
-        turn, unit = near_turn(i, LAGS[1])
-
-        @pl.when(turn)
-        def _(unit=unit):
-            at_middle_second(unit, near_z, r.z_in)
-
-        turn, unit = near_turn(i, LAGS[2])
-
-        @pl.when(turn)
-        def _(unit=unit):
-            def action(here):
-                r.staged[unit] = gathered(unit, here, near_z, r.z_in)
-
-            everywhere(action)
-
         @pl.when(i == 1)
         def _():
             norm_to_pair().wait()
@@ -722,7 +791,7 @@
             for hop in (1, 2, 3):
                 norm_to_z(hop).start()
 
-        @pl.when(i == 18)
+        @pl.when(i == 15)
         def _():
             for hop in (1, 2, 3):
                 norm_to_z(hop).wait_recv()
@@ -730,7 +799,7 @@
 
         return carry
 
-    lax.fori_loop(0, max(NEAR + LAGS[2], *(step + 1 for step in FAR_DONE)), advance, 0)
+    lax.fori_loop(0, NEAR + LAGS[2], advance, 0)
 
     norm_to_y().wait_send()
     for hop in (1, 2, 3):
@@ -738,6 +807,10 @@
     share_acts(1).wait_send()
     for micro in range(2):
         share_branch(micro).wait_send()
+        branch_across(micro).wait_send()
+        branch_onward(micro).wait_send()
+        for peer in range(3):
+            share_quad(micro, peer).wait_send()
         share_lifted(micro).wait_send()
         share_rest(micro).wait_send()
 
@@ -749,13 +822,18 @@
         def _():
             relay_back(micro).wait_send()
 
-    def drain_near(near, carry):
-        to_y(FAR + near).wait_send()
+    def drain_y(near, carry):
+        to_y(QUAD + near).wait_send()
+        return carry
+
+    lax.fori_loop(0, NEAR, drain_y, 0)
+
+    def drain_z(unit, carry):
         for lane in range(3):
-            near_z(FAR + near, 0, 0, lane, dp).wait_send()
+            near_z(unit, 0, 0, lane, dp).wait_send()
         return carry
 
-    lax.fori_loop(0, NEAR, drain_near, 0)
+    lax.fori_loop(FAR, UNITS, drain_z, 0)
 
     def drain_far(unit, carry):
         far_to_y(unit, 0).wait_send()
@@ -776,7 +854,7 @@
         return copy
 
     copies = [start(result, out_result.at[0, :, 0]), start(grad, out_grad.at[0, :, 0])]
-    for slot, piece in enumerate(PIECES):
+    for piece in range(UNITS):
         half = pl.ds(piece % 2 * COLUMNS, COLUMNS)
         if piece < 8:
             target = out_down.at[0, pl.ds(piece // 2 * BLOCK, BLOCK), half]
@@ -786,7 +864,7 @@
             target = out_outward.at[0, :, half]
         else:
             target = out_inward.at[0, :, pl.ds((piece - 18) * COLUMNS, COLUMNS)]
-        copies.append(start(staged.at[slot], target))
+        copies.append(start(staged.at[piece], target))
     share = gain_grad.shape[2]
     for index in range(width // share):
 
@@ -825,26 +903,28 @@
             pltpu.VMEM((width, width), SLIM),
             pltpu.VMEM((width, wide_ff), SLIM),
             pltpu.VMEM((wide_ff, width), SLIM),
-            pltpu.VMEM((9, 4 * length, width), SLIM),
-            pltpu.VMEM((7, 8 * BLOCK, 4 * length), SLIM),
-            pltpu.VMEM((7, 8 * BLOCK, length), SLIM),
+            pltpu.VMEM((8, 4 * length, width), SLIM),
+            pltpu.VMEM((8 * length, width), SLIM),
+            pltpu.VMEM((4, 8 * BLOCK, 4 * length), SLIM),
+            pltpu.VMEM((4, 8 * BLOCK, length), SLIM),
+            pltpu.VMEM((3, 4 * BLOCK, 8 * length), SLIM),
+            pltpu.VMEM((2, 3, 3, 4 * BLOCK, length), SLIM),
             pltpu.VMEM((2, width // HEAD, length, length), SLIM),
             pltpu.VMEM((length, width), SLIM),
             pltpu.VMEM((length, width), SLIM),
             pltpu.VMEM((width, length), SLIM),
             pltpu.VMEM((length, width), WIDE),
-            pltpu.VMEM((2, length, width), SLIM),
             pltpu.VMEM((4, 8, width), WIDE),
             pltpu.VMEM((length, length), WIDE),
             pltpu.VMEM((UNITS, 2, 4 * BLOCK, COLUMNS), SLIM),
             pltpu.VMEM((NEAR, 4 * BLOCK, COLUMNS), SLIM),
-            pltpu.VMEM((NEAR, 5, BLOCK, COLUMNS), SLIM),
+            pltpu.VMEM((UNITS - FAR, 5, BLOCK, COLUMNS), SLIM),
             pltpu.VMEM((FAR, BLOCK, COLUMNS), SLIM),
             pltpu.VMEM((FAR, 5, 2, BLOCK, COLUMNS), SLIM),
             pltpu.VMEM((8, 8, width), WIDE),
             dma((4,)), dma((2,)),
-            *[dma((2,))] * 10, pltpu.SemaphoreType.REGULAR,
-            dma((NEAR,)), dma((NEAR,)), dma((NEAR, 3)), dma((NEAR, 5)),
+            *[dma((2,))] * 8, *[dma((2,))] * 4, dma((2, 3)), dma((2, 3)), *[dma((2,))] * 2, pltpu.SemaphoreType.REGULAR,
+            dma((NEAR,)), dma((NEAR,)), dma((UNITS - FAR, 3)), dma((UNITS - FAR, 5)),
             dma((FAR,)), dma((FAR,)), dma((FAR, 3)), dma((FAR, 5)), dma((5,)), dma((5,)),
         ],
         compiler_params=pltpu.CompilerParams(

time: 149 us -> 147 us (0.987)
  Pallas kernels: 148 us -> 146 us
    pallas_call x1, Pallas kernels: 145 us -> 144 us  [step_on_device(): pl.pallas_call(step_kernel, out_shape=(pltpu.VMEM((2, length, width), SLI...]
where the time goes in v6:
time: 147 us
  Pallas kernels  146 us (99%)
    pallas_call x1, Pallas kernels, step_on_device(): pl.pallas_call(step_kernel, out_shape=(pltpu.VMEM((2, length, width), SLI...  144 us

profile of v6, /device:TPU:0, one launch (start us, length us, event | category | flops | bytes accessed | tf_op | source)
XLA Modules:
  0.0 147.0 jit_solution(16521129349397693475)
XLA Ops:
  0.6 143.6 %shard_map.161 = (bf16[2,256,768]{2,1,0:T(8,128)(2,1)S(1)}, f32[2,256,768]{2,1,0:T(8,128)S(1)}, f32[24,48,384]{2,1,0:T(8,128)S(1)}, f32[8,768]{1,0:T(8,128)S(1)}) custom-call(bf16[2,1,256,768]{3,2,1,0:T(8,128)(2,1)} %refs_0_.1, bf16[2,1,256,768]{3,2,1,0:T(8,128)(2,1)} %refs_1_.1, bf16[1,768,2304]{2,1,0:T(8,128)(2,1)} %refs_2_.1, ...), custom_call_target="tpu_custom_call" | custom-call | tf_op jit(solution)/shard_map/pallas_call | solution.py:890
  144.3 2.5 %shard_map.162 = (bf16[1,2,1,256,768]{4,3,2,1,0:T(8,128)(2,1)}, f32[1,2,1,256,768]{4,3,2,1,0:T(8,128)}, f32[1,48,2304]{2,1,0:T(8,128)}, f32[1,48,768]{2,1,0:T(8,...) custom-call(bf16[2,256,768]{2,1,0:T(8,128)(2,1)S(1)} %get-tuple-element.12.re, ...), custom_call_target="tpu_custom_call" | custom-call | tf_op jit(solution)/shard_map/pallas_call | solution.py:938

commit v7 on v6

--- a/solution.py
+++ b/solution.py
@@ -106,7 +106,6 @@
 def forward(r, micro, tok, first, leading):
     length, width = r.normed.shape
     tokens = pl.ds(tok, length)
-    mask_bias(r, micro)
     r.normed[...] = norm_rows_bf16(r, r.stream[micro].astype(WIDE), 0)
 
     @pl.when(first)
@@ -237,6 +236,7 @@
         r.grads[part, tokens, :] = lifted_grad
         r.total[...] += times_turned(lifted_grad, r.up[:, cols])
     r.share_lifted(micro).start()
+    r.between(micro)
     middle_grad = r.branch[r.quad_rows(micro), :].astype(WIDE) + norm_backward(
         r, r.middle[micro], r.total[...], 1
     )
@@ -533,12 +533,26 @@
             def _():
                 action(here)
 
+    def far_units():
+        for micro in range(2):
+            share_branch(micro, 1 - c).wait_recv()
+            share_acts(micro, 1 - c).wait_recv()
+
+        def body(unit, carry):
+            far_unit(unit)
+            return carry
+
+        lax.fori_loop(0, FAR, body, 0)
+        branch_across(0, 1 - y).wait_recv()
+        branch_onward(0).start()
+
+    r.between = lambda micro: pl.when(leading & (micro == 1))(far_units)
+
     def slot(t, carry):
         trailing = jnp.logical_not(leading)
         half = lax.div(t, 2)
         is_forward = (leading & (t < 2)) | (trailing & ((t == 1) | (t == 3)))
         is_backward = (leading & ((t == 3) | (t == 5))) | (trailing & ((t == 2) | (t == 4)))
-        is_weights = (leading & (t == 4)) | (trailing & (t == 5))
 
         @pl.when(trailing & (t == 0))
         def _():
@@ -552,6 +566,8 @@
         def _():
             micro = jnp.where(leading, jnp.minimum(t, 1), jnp.minimum(half, 1))
 
+            mask_bias(r, micro)
+
             @pl.when(leading)
             def _():
                 load_x(micro).wait()
@@ -615,18 +631,7 @@
         def _():
             arrive(1)
 
-        @pl.when(is_weights)
-        def _():
-            for micro in range(2):
-                share_branch(micro, 1 - c).wait_recv()
-                share_acts(micro, 1 - c).wait_recv()
-
-            def body(unit, carry):
-                far_unit(unit)
-                return carry
-
-            lax.fori_loop(0, FAR, body, 0)
-
+        pl.when(trailing & (t == 5))(far_units)
         return carry
 
     lax.fori_loop(0, 6, slot, 0)
@@ -653,9 +658,8 @@
         return carry
 
     lax.fori_loop(0, EARLY_NEAR, early_near, 0)
-    for micro in range(2):
-        branch_across(micro, 1 - y).wait_recv()
-        branch_onward(micro).start()
+    branch_across(1, 1 - y).wait_recv()
+    branch_onward(1).start()
     for micro in range(2):
         branch_onward(micro, 1 - c).wait_recv()
         for peer in range(3):

time: 147 us -> 145 us (0.986)
  Pallas kernels: 146 us -> 144 us
    pallas_call x1, Pallas kernels: 144 us -> 142 us  [step_on_device(): pl.pallas_call(step_kernel, out_shape=(pltpu.VMEM((2, length, width), SLI...]
where the time goes in v7:
time: 145 us
  Pallas kernels  144 us (99%)
    pallas_call x1, Pallas kernels, step_on_device(): pl.pallas_call(step_kernel, out_shape=(pltpu.VMEM((2, length, width), SLI...  142 us

profile of v7, /device:TPU:0, one launch (start us, length us, event | category | flops | bytes accessed | tf_op | source)
XLA Modules:
  0.0 145.2 jit_solution(9781574471992655784)
XLA Ops:
  0.6 141.8 %shard_map.161 = (bf16[2,256,768]{2,1,0:T(8,128)(2,1)S(1)}, f32[2,256,768]{2,1,0:T(8,128)S(1)}, f32[24,48,384]{2,1,0:T(8,128)S(1)}, f32[8,768]{1,0:T(8,128)S(1)}) custom-call(bf16[2,1,256,768]{3,2,1,0:T(8,128)(2,1)} %refs_0_.1, bf16[2,1,256,768]{3,2,1,0:T(8,128)(2,1)} %refs_1_.1, bf16[1,768,2304]{2,1,0:T(8,128)(2,1)} %refs_2_.1, ...), custom_call_target="tpu_custom_call" | custom-call | tf_op jit(solution)/shard_map/pallas_call | solution.py:894
  142.5 2.5 %shard_map.162 = (bf16[1,2,1,256,768]{4,3,2,1,0:T(8,128)(2,1)}, f32[1,2,1,256,768]{4,3,2,1,0:T(8,128)}, f32[1,48,2304]{2,1,0:T(8,128)}, f32[1,48,768]{2,1,0:T(8,...) custom-call(bf16[2,256,768]{2,1,0:T(8,128)(2,1)S(1)} %get-tuple-element.12.re, ...), custom_call_target="tpu_custom_call" | custom-call | tf_op jit(solution)/shard_map/pallas_call | solution.py:942

commit v8 on v7

--- a/solution.py
+++ b/solution.py
@@ -21,8 +21,8 @@
 NEAR = UNITS - QUAD
 BLOCK = 48
 COLUMNS = 384
-EARLY_NEAR = 2
-HOLD = 0
+EARLY_NEAR = 3
+HOLD = 1
 LAGS = (2, 4, 6)
 FAR_FIRST = (0, 5)
 FAR_SECOND = (2, 9)

time: 145 us -> 145 us (level)
  no operation moved by 1% of the time
where the time goes in v8:
time: 145 us
  Pallas kernels  144 us (99%)
    pallas_call x1, Pallas kernels, step_on_device(): pl.pallas_call(step_kernel, out_shape=(pltpu.VMEM((2, length, width), SLI...  141 us

profile of v8, /device:TPU:0, one launch (start us, length us, event | category | flops | bytes accessed | tf_op | source)
XLA Modules:
  0.0 144.8 jit_solution(5600353967773564321)
XLA Ops:
  0.6 141.5 %shard_map.161 = (bf16[2,256,768]{2,1,0:T(8,128)(2,1)S(1)}, f32[2,256,768]{2,1,0:T(8,128)S(1)}, f32[24,48,384]{2,1,0:T(8,128)S(1)}, f32[8,768]{1,0:T(8,128)S(1)}) custom-call(bf16[2,1,256,768]{3,2,1,0:T(8,128)(2,1)} %refs_0_.1, bf16[2,1,256,768]{3,2,1,0:T(8,128)(2,1)} %refs_1_.1, bf16[1,768,2304]{2,1,0:T(8,128)(2,1)} %refs_2_.1, ...), custom_call_target="tpu_custom_call" | custom-call | tf_op jit(solution)/shard_map/pallas_call | solution.py:894
  142.1 2.5 %shard_map.162 = (bf16[1,2,1,256,768]{4,3,2,1,0:T(8,128)(2,1)}, f32[1,2,1,256,768]{4,3,2,1,0:T(8,128)}, f32[1,48,2304]{2,1,0:T(8,128)}, f32[1,48,768]{2,1,0:T(8,...) custom-call(bf16[2,256,768]{2,1,0:T(8,128)(2,1)S(1)} %get-tuple-element.12.re, ...), custom_call_target="tpu_custom_call" | custom-call | tf_op jit(solution)/shard_map/pallas_call | solution.py:942

commit v9 on v8

--- a/solution.py
+++ b/solution.py
@@ -22,7 +22,7 @@
 BLOCK = 48
 COLUMNS = 384
 EARLY_NEAR = 3
-HOLD = 1
+HOLD = 0
 LAGS = (2, 4, 6)
 FAR_FIRST = (0, 5)
 FAR_SECOND = (2, 9)

time: 145 us -> 145 us (level)
  no operation moved by 1% of the time
where the time goes in v9:
time: 145 us
  Pallas kernels  144 us (99%)
    pallas_call x1, Pallas kernels, step_on_device(): pl.pallas_call(step_kernel, out_shape=(pltpu.VMEM((2, length, width), SLI...  141 us

profile of v9, /device:TPU:0, one launch (start us, length us, event | category | flops | bytes accessed | tf_op | source)
XLA Modules:
  0.0 144.8 jit_solution(6835971020473299498)
XLA Ops:
  0.6 141.5 %shard_map.161 = (bf16[2,256,768]{2,1,0:T(8,128)(2,1)S(1)}, f32[2,256,768]{2,1,0:T(8,128)S(1)}, f32[24,48,384]{2,1,0:T(8,128)S(1)}, f32[8,768]{1,0:T(8,128)S(1)}) custom-call(bf16[2,1,256,768]{3,2,1,0:T(8,128)(2,1)} %refs_0_.1, bf16[2,1,256,768]{3,2,1,0:T(8,128)(2,1)} %refs_1_.1, bf16[1,768,2304]{2,1,0:T(8,128)(2,1)} %refs_2_.1, ...), custom_call_target="tpu_custom_call" | custom-call | tf_op jit(solution)/shard_map/pallas_call | solution.py:894
  142.1 2.5 %shard_map.162 = (bf16[1,2,1,256,768]{4,3,2,1,0:T(8,128)(2,1)}, f32[1,2,1,256,768]{4,3,2,1,0:T(8,128)}, f32[1,48,2304]{2,1,0:T(8,128)}, f32[1,48,768]{2,1,0:T(8,...) custom-call(bf16[2,256,768]{2,1,0:T(8,128)(2,1)S(1)} %get-tuple-element.12.re, ...), custom_call_target="tpu_custom_call" | custom-call | tf_op jit(solution)/shard_map/pallas_call | solution.py:942
